TPU v7x, 256 devices: a whole 4x4x8 slice. The times are simulated.
256 devices in a mesh: mem: 16 (over x, y_lo, core), lat: 16 (over y_hi, z).
Axes of the slice: x: 4, y: 4 (y_hi: 2, y_lo: 2; y = y_hi * 2 + y_lo), z: 8, core: 2. Of those that a mesh axis runs over, the one named last changes fastest.
Arguments:
- state: float32 [16, 641, 32, 160], P('mem', None, 'lat'), may hold values from -6 to 6
- conv_kernel: float32 [25, 641], replicated, may hold values from -1.25 to 1.25
- norm_gain: float32 [641], replicated, may hold values from 0.5 to 1.5
- up_weight: bfloat16 [641, 1282], replicated, may hold values from -0.25 to 0.25
- down_weight: bfloat16 [1282, 641], replicated, may hold values from -0.15625 to 0.15625
- field_head_weight: bfloat16 [641, 72], replicated, may hold values from -0.25 to 0.25
- target: float32 [72, 32, 160], P(None, 'lat'), may hold values from -9 to 9
- field_weight: float32 [72], replicated, may hold values from 0.3 to 3
Outputs:
- loss: float32 [], replicated
- grad_kernel: float32 [25, 641], replicated
- grad_gain: float32 [641], replicated
- grad_up: float32 [641, 1282], replicated
- grad_down: float32 [1282, 641], replicated
- grad_head: float32 [641, 72], replicated
All inputs are finite; a program needn't handle non-finite values.
Results may differ from a plain program's by a relative error of at most 0.005.
The roundings to bfloat16 on the way count: a program that leaves them out, or rounds other values in their place, can miss the bound.
Values may be sent and summed in bfloat16 or wider, within the bound.
A program may use at most 128 MiB of HBM per device.

v0:
```python
import functools
import math

import jax
import jax.numpy as jnp
from jax import lax
from jax.sharding import Mesh
from jax.sharding import PartitionSpec as P

MEM = ("mem_0", "mem_1", "mem_2")
LAT = ("lat_0", "lat_1")
MEM_LAT = ("mem_0", "mem_1", "mem_2", "lat_0", "lat_1")


DELTA = 0.1
EPSILON = 1e-05


def extended(cells, sides, width):
    for axis, dim in sides:
        count = lax.axis_size(axis)
        ends = count - 1
        head = lax.slice_in_dim(cells, 0, width, axis=dim)
        tail = lax.slice_in_dim(cells, cells.shape[dim] - width, cells.shape[dim], axis=dim)
        cells = jnp.concatenate(
            [
                lax.ppermute(tail, axis, [(i, (i + 1) % count) for i in range(ends)]),
                cells,
                lax.ppermute(head, axis, [((i + 1) % count, i) for i in range(ends)]),
            ],
            axis=dim,
        )
    return cells


def cut_along(shard, dim, count):
    shape = shard.shape
    pieces = shard.reshape(*shape[:dim], count, shape[dim] // count, *shape[dim + 1 :])
    return jnp.moveaxis(pieces, dim, 0)


def joined_along(pieces, dim):
    pieces = jnp.moveaxis(pieces, 0, dim)
    shape = pieces.shape
    return pieces.reshape(*shape[:dim], shape[dim] * shape[dim + 1], *shape[dim + 2 :])


def moved_by_axis(pieces, axes, sequence):
    shape = [lax.axis_size(a) for a in axes]
    pieces = pieces.reshape(*shape, *pieces.shape[1:])
    for k in sequence:
        pieces = lax.all_to_all(pieces, axes[k], split_axis=k, concat_axis=k, tiled=True)
    return pieces.reshape(-1, *pieces.shape[len(axes) :])


def core_and_chips(shard, groups, sequence, split_dim, concat_dim):
    count = lax.axis_size(groups[0]) * lax.axis_size(groups[1])
    pieces = cut_along(shard, split_dim, count)
    return joined_along(moved_by_axis(pieces, groups, sequence), concat_dim)


def one_axis_at_a_time(shard, axes):
    return functools.reduce(lax.psum, axes, shard)


def packed_total(arrays, axis):
    line, at, done = (jnp.concatenate([a.reshape(-1) for a in arrays]), 0, [])
    total = lax.psum(line, axis)
    for a in arrays:
        done.append(total[at : at + a.size].reshape(a.shape))
        at += a.size
    return tuple(done)


def softened_absolute(diff):
    return jnp.sqrt(diff * diff + DELTA * DELTA) - DELTA


def softened_derivative(diff):
    return diff / jnp.sqrt(diff * diff + DELTA * DELTA)


def gelu_parts(before_activation):
    cumul = 0.5 * (1.0 + jax.scipy.special.erf(before_activation / math.sqrt(2.0)))
    density = jnp.exp(-0.5 * before_activation * before_activation) / math.sqrt(2.0 * math.pi)
    return (before_activation * cumul, cumul + before_activation * density)


def leading_product(left, right):
    return lax.dot_general(
        left, right, (((0,), (0,)), ((), ())), preferred_element_type=jnp.float32
    )


def tail_dot(left, right):
    return lax.dot_general(
        left, right, (((1,), (1,)), ((), ())), preferred_element_type=jnp.float32
    )


def stencil(window, kernel, height):
    result = jnp.zeros((window.shape[0], height, window.shape[2]), jnp.float32)
    for col_off in range(5):
        shifted = jnp.roll(window, 2 - col_off, axis=2)
        for row_off in range(5):
            result = (
                result
                + kernel[row_off * 5 + col_off][:, None, None]
                * shifted[:, row_off : row_off + height]
            )
    return result


def kernel_grad(window, upstream, height):
    terms = [None] * 25
    for col_off in range(5):
        shifted = jnp.roll(window, 2 - col_off, axis=2)
        for row_off in range(5):
            terms[row_off * 5 + col_off] = jnp.sum(
                upstream * shifted[:, row_off : row_off + height], axis=(1, 2)
            )
    return jnp.stack(terms)


def forward_apply(field, window, kernel, gain, up_weight, down_weight, field_head_weight):
    height = field.shape[1]
    channels = field.shape[0]
    summed = (field + stencil(window, kernel, height)).reshape(channels, -1)
    center = summed - jnp.mean(summed, axis=0)
    inverse_norm = lax.rsqrt(jnp.mean(center * center, axis=0) + EPSILON)
    normalized_input = center * inverse_norm
    gain_scaled = (normalized_input * gain[:, None]).astype(jnp.bfloat16)
    before_activation = leading_product(up_weight, gain_scaled)
    activ, unused = gelu_parts(before_activation)
    hidden_activation = activ.astype(jnp.bfloat16)
    output = summed + leading_product(down_weight, hidden_activation)
    rounded_values = output.astype(jnp.bfloat16)
    member_prediction = leading_product(field_head_weight, rounded_values)
    return (
        member_prediction,
        (
            normalized_input,
            inverse_norm,
            gain_scaled,
            before_activation,
            hidden_activation,
            rounded_values,
        ),
    )


def backward(window, stored_residuals, cotangent, gain, up_weight, down_weight, field_head_weight):
    (
        normalized_input,
        inverse_norm,
        gain_scaled,
        before_activation,
        hidden_activation,
        rounded_values,
    ) = stored_residuals
    height = window.shape[1] - 4
    grad_head = tail_dot(rounded_values, cotangent)
    d_output = jnp.dot(field_head_weight, cotangent, preferred_element_type=jnp.float32)
    d_round = d_output.astype(jnp.bfloat16)
    grad_down = tail_dot(hidden_activation, d_round)
    d_hidden = jnp.dot(down_weight, d_round, preferred_element_type=jnp.float32)
    unused, slope = gelu_parts(before_activation)
    d_preact = (d_hidden * slope).astype(jnp.bfloat16)
    grad_up = tail_dot(gain_scaled, d_preact)
    d_scaled = jnp.dot(up_weight, d_preact, preferred_element_type=jnp.float32)
    grad_gain = jnp.sum(d_scaled * normalized_input, axis=1)
    d_normed = d_scaled * gain[:, None]
    d_summed = d_output + inverse_norm * (
        d_normed
        - jnp.mean(d_normed, axis=0)
        - normalized_input * jnp.mean(d_normed * normalized_input, axis=0)
    )
    upstream = d_summed.reshape(window.shape[0], height, window.shape[2])
    grad_kernel = kernel_grad(window, upstream, height)
    return (grad_kernel, grad_gain, grad_up, grad_down, grad_head)


def local(
    state, conv_kernel, norm_gain, up_weight, down_weight, field_head_weight, target, field_weight
):
    field = state[0]
    member_states = lax.axis_size(MEM)
    height = field.shape[1]
    nlat = lax.axis_size(LAT) * height
    width = field.shape[2]
    nfields = target.shape[0]
    window = extended(field, ((LAT, 1),), 2)
    member_prediction, stored_residuals = forward_apply(
        field, window, conv_kernel, norm_gain, up_weight, down_weight, field_head_weight
    )
    grid_cell_values = member_prediction.shape[1]
    observed_target = target.reshape(nfields, grid_cell_values)
    row_float = (lax.axis_index(LAT) * height + jnp.arange(height)).astype(jnp.float32)
    area_rows = jnp.cos(0.5 * math.pi * ((row_float + 0.5) / nlat - 1.0))
    area = jnp.repeat(area_rows, width)
    member_count = nlat * width * nfields
    scale_grad = 1.0 / (member_states * math.sqrt(member_count))
    pair_norm = 2.0 * member_states * (member_states - 1)
    block = grid_cell_values // member_states
    outgoing = member_prediction.reshape(1, nfields, member_states, block)
    gathered_members = core_and_chips(
        outgoing, (("mem_0", "mem_1"), "mem_2"), (1, 0), 2, 0
    ).reshape(member_states, nfields, block)
    mine = lax.axis_index(MEM)
    truth_block = lax.dynamic_index_in_dim(
        observed_target.reshape(nfields, member_states, block), mine, 1, keepdims=False
    )
    area_block = lax.dynamic_index_in_dim(
        area.reshape(member_states, block), mine, 0, keepdims=False
    )
    differences = gathered_members[:, None] - gathered_members[None]
    ensemble_spread = (
        jnp.mean(softened_absolute(gathered_members - truth_block[None]), axis=0)
        - jnp.sum(softened_absolute(differences), axis=(0, 1)) / pair_norm
    )
    partial_value = jnp.sum(field_weight[:, None] * area_block[None, :] * ensemble_spread)
    loss = one_axis_at_a_time(partial_value, MEM_LAT) / member_count
    pairwise_derivatives = jnp.sum(softened_derivative(differences), axis=1)
    member_cot = (
        field_weight[None, :, None]
        * area_block[None, None, :]
        * (
            softened_derivative(gathered_members - truth_block[None])
            - pairwise_derivatives / (member_states - 1)
        )
        * scale_grad
    )
    cot_rounded = member_cot.astype(jnp.bfloat16).reshape(member_states, nfields, 1, block)
    returned = core_and_chips(cot_rounded, (("mem_0", "mem_1"), "mem_2"), (1, 0), 0, 2)
    cotangent = returned.reshape(nfields, grid_cell_values)
    grads = backward(
        window, stored_residuals, cotangent, norm_gain, up_weight, down_weight, field_head_weight
    )
    totals = packed_total((grads[0], grads[1], grads[2], grads[3], grads[4]), MEM_LAT)
    return (loss, totals[0], totals[1], totals[2], totals[3], totals[4])


def solution(mesh):
    finer = Mesh(mesh.devices.reshape(4, 2, 2, 2, 8), ("mem_0", "mem_1", "mem_2", "lat_0", "lat_1"))
    in_specs = (P(MEM, None, LAT, None), P(), P(), P(), P(), P(), P(None, LAT, None), P())
    out_specs = (P(), P(), P(), P(), P(), P())
    return jax.shard_map(local, mesh=finer, in_specs=in_specs, out_specs=out_specs, check_vma=False)
```

profile of v0, /device:TPU:1, one launch (start us, length us, event | category | flops | bytes accessed | tf_op | source)
XLA Modules:
  0.0 502.1 jit_solution(14818053159749364290)
XLA Ops:
  8.6 6.0 %collective-permute-start = (f32[641,2,160]{0,2,1:T(8,128)}, f32[641,2,160]{0,2,1:T(8,128)}, u32[]{:S(2)}, u32[]{:S(2)}) collective-permute-start(f32[641,2,160]{0,2,1:T(8,128)} %bitcast.64), channel_id=1, source_target_pairs={{0,1},{1,2},{2,3},{3,4},{4,5},{5,6},{6,7},{7,8},{8,9},{9,10},{10,1... | collective-permute-start | bytes 2461448 | tf_op jit(solution)/shard_map/ppermute | solution.py:27
  20.8 10.7 %collective-permute-done.1 = f32[641,2,160]{0,2,1:T(8,128)S(1)} collective-permute-done((f32[641,2,160]{0,2,1:T(8,128)}, f32[641,2,160]{0,2,1:T(8,128)S(1)}, u32[]{:S(2)}, u32[]{:S(2)}) %collective-permute-start.1) | collective-permute-done | bytes 820512 | tf_op jit(solution)/shard_map/ppermute | solution.py:29
  39.4 4.6 fusion.3
  44.1 5.9 %fusion.26 = (f32[2,160]{1,0:T(2,128)S(1)}, f32[641,2,160]{0,2,1:T(8,128)}) fusion(f32[641,2,160]{0,2,1:T(8,128)S(1)} %bitcast.67, f32[641,6,160]{0,2,1:T(8,128)S(1)} %get-tuple-element.112, f32[641]{0:T(1024)S(1)} %get-tuple-element.102, f32[641]{0:T(1024)S(1)} %get-tuple-element.103, f32[641]{0:T(1024)S(1)} %get-tuple-element.80, ...), kind=kLoop, calls=%fused_computation.119 | loop fusion | flops 10871040 | bytes 19756900 | tf_op jit(solution)/shard_map/reduce_sum | solution.py:129
  58.8 6.9 %all_to_all.20 = f32[8,2,1,72,1,20]{3,0,5,4,2,1:T(8,128)S(1)} all-to-all(f32[8,2,1,72,1,20]{3,0,5,4,2,1:T(8,128)S(1)} %copy.70), channel_id=1, replica_groups=mesh['mem_0'=4,'mem_1'=2,'mem_2'=2,'lat_0'=2,'lat_1'=8] {'mem_2'}, dimensions={1} | all-to-all | bytes 184320 | tf_op jit(solution)/shard_map/all_to_all | solution.py:52
  66.5 5.0 %all-to-all-start.1 = ((f32[8,2,1,72,1,20]{3,1,5,4,2,0:T(2,128)}), f32[8,2,1,72,1,20]{3,1,5,4,2,0:T(2,128)S(1)}, u32[]{:S(2)}, u32[]{:S(2)}) async-start(f32[8,2,1,72,1,20]{3,1,5,4,2,0:T(2,128)} %copy.71), calls=%async_computation.1 | async-start | bytes 327680 | tf_op jit(solution)/shard_map/all_to_all | solution.py:52
  72.3 4.8 all-to-all-done.1
  79.6 5.1 %all_to_all.21 = bf16[8,2,1,72,1,20]{3,0,5,4,2,1:T(8,128)(2,1)S(1)} all-to-all(bf16[8,2,1,72,1,20]{3,0,5,4,2,1:T(8,128)(2,1)S(1)} %get-tuple-element.118), channel_id=1, replica_groups=mesh['mem_0'=4,'mem_1'=2,'mem_2'=2,'lat_0'=2,'lat_1'=8] {'mem_2'}, dimensions={1} | all-to-all | bytes 92160 | tf_op jit(solution)/shard_map/all_to_all | solution.py:52
  84.8 7.6 %all_to_all.22 = bf16[8,2,1,72,1,20]{3,1,5,4,2,0:T(2,128)(2,1)S(1)} all-to-all(bf16[8,2,1,72,1,20]{3,1,5,4,2,0:T(2,128)(2,1)S(1)} %copy.79), channel_id=1, replica_groups=mesh['mem_0'=4,'mem_1'=2,'mem_2'=2,'lat_0'=2,'lat_1'=8] {'mem_0','mem_1'}, dimensions={0} | all-to-all | bytes 92160 | tf_op jit(solution)/shard_map/all_to_all | solution.py:52
  93.6 3.3 fusion.5
  101.2 3.2 fusion.19
  112.3 5.3 %reshape.171 = f32[821762]{0:T(1024)} reshape(f32[641,1282]{1,0:T(8,128)} %fusion.22) | data formatting | bytes 6574096 | tf_op jit(solution)/shard_map/reshape | solution.py:67
  117.6 5.6 %reshape.172 = f32[821762]{0:T(1024)} reshape(f32[1282,641]{1,0:T(8,128)} %fusion.19) | data formatting | bytes 6574096 | tf_op jit(solution)/shard_map/reshape | solution.py:67
  123.4 59.2 %concatenate.39 = f32[1706342]{0:T(1024)} concatenate(f32[16025]{0:T(1024)S(1)} %reshape.170, f32[641]{0:T(1024)S(1)} %get-tuple-element.56, f32[821762]{0:T(1024)} %reshape.171, f32[821762]{0:T(1024)} %reshape.172, f32[46152]{0:T(1024)S(1)} %reshape.173), dimensions={0} | concatenate | bytes 13650736 | tf_op jit(solution)/shard_map/concatenate | solution.py:67
  183.2 7.5 %psum.42 = f32[]{:T(128)} all-reduce(f32[]{:T(128)} %multiply_reduce_fusion.28), channel_id=1, replica_groups=mesh['mem_0'=4,'mem_1'=2,'mem_2'=2,'lat_0'=2,'lat_1'=8] {'mem_0'}, use_global_device_ids=true, to_apply=%region_5.6 | all-reduce | flops 1 | bytes 8 | tf_op jit(solution)/shard_map/psum | solution.py:63
  190.7 4.4 psum.43
  195.1 7.7 %psum.44 = f32[]{:T(128)} all-reduce(f32[]{:T(128)} %psum.43), channel_id=1, replica_groups=mesh['mem_0'=4,'mem_1'=2,'mem_2'=2,'lat_0'=2,'lat_1'=8] {'mem_2'}, use_global_device_ids=true, to_apply=%region_7.8 | all-reduce | flops 1 | bytes 8 | tf_op jit(solution)/shard_map/psum | solution.py:63
  202.8 15.9 %psum.45 = f32[]{:T(128)} all-reduce(f32[]{:T(128)} %psum.44), channel_id=1, replica_groups=mesh['mem_0'=4,'mem_1'=2,'mem_2'=2,'lat_0'=2,'lat_1'=8] {'lat_0'}, use_global_device_ids=true, to_apply=%region_8.9 | all-reduce | flops 1 | bytes 8 | tf_op jit(solution)/shard_map/psum | solution.py:63
  218.7 12.2 %psum.46 = f32[]{:T(128)} all-reduce(f32[]{:T(128)} %psum.45), channel_id=1, replica_groups=mesh['mem_0'=4,'mem_1'=2,'mem_2'=2,'lat_0'=2,'lat_1'=8] {'lat_1'}, use_global_device_ids=true, to_apply=%region_9.10 | all-reduce | flops 1 | bytes 8 | tf_op jit(solution)/shard_map/psum | solution.py:63
  231.6 231.2 %all-reduce.2.cloned.1.call-done = f32[1706342]{0:T(1024)} async-done(((f32[1706342]{0:T(1024)}), f32[1706342]{0:T(1024)}) %all-reduce.2.cloned.1.call-update) | async-done | bytes 6825384 | tf_op jit(solution)/shard_map/psum | solution.py:68
  464.5 7.5 %fusion.27 = (f32[821762]{0:T(1024)}, f32[821762]{0:T(1024)}) fusion(f32[1706342]{0:T(1024)} %all-reduce.2.cloned.1.call-done), kind=kLoop, calls=%fused_computation.120 | loop fusion | bytes 13148192 | tf_op jit(solution)/shard_map/slice | solution.py:70
  471.9 6.2 %reshape.175 = f32[641,1282]{1,0:T(8,128)} reshape(f32[821762]{0:T(1024)} %get-tuple-element.109) | data formatting | bytes 6574096 | tf_op jit(solution)/shard_map/reshape | solution.py:70
  478.1 7.1 %reshape.176 = f32[1282,641]{1,0:T(8,128)} reshape(f32[821762]{0:T(1024)} %get-tuple-element.108) | data formatting | bytes 6574096 | tf_op jit(solution)/shard_map/reshape | solution.py:70
  485.2 5.4 %copy.84 = f32[1282,641]{0,1:T(8,128)} copy(f32[1282,641]{1,0:T(8,128)} %reshape.176) | data formatting | bytes 6574096
  (128 shorter events, 47.4 us)
Async XLA Ops:
  7.2 45.9 %copy-start = (bf16[641,1282]{1,0:T(8,128)(2,1)S(1)}, bf16[641,1282]{1,0:T(8,128)(2,1)}, u32[]{:S(2)}) copy-start(bf16[641,1282]{1,0:T(8,128)(2,1)} %param.11) | copy-start | bytes 4930576
  7.2 24.3 %collective-permute-start.1 = (f32[641,2,160]{0,2,1:T(8,128)}, f32[641,2,160]{0,2,1:T(8,128)S(1)}, u32[]{:S(2)}, u32[]{:S(2)}) collective-permute-start(f32[641,2,160]{0,2,1:T(8,128)} %bitcast.63), channel_id=1, source_target_pairs={{1,0},{2,1},{3,2},{4,3},{5,4},{6,5},{7,6},{8,7},{9,8},{10,9},{11,1... | collective-permute-start | bytes 2461448 | tf_op jit(solution)/shard_map/ppermute | solution.py:29
  8.6 23.9 %collective-permute-start = (f32[641,2,160]{0,2,1:T(8,128)}, f32[641,2,160]{0,2,1:T(8,128)}, u32[]{:S(2)}, u32[]{:S(2)}) collective-permute-start(f32[641,2,160]{0,2,1:T(8,128)} %bitcast.64), channel_id=1, source_target_pairs={{0,1},{1,2},{2,3},{3,4},{4,5},{5,6},{6,7},{7,8},{8,9},{9,10},{10,1... | collective-permute-start | bytes 2461448 | tf_op jit(solution)/shard_map/ppermute | solution.py:27
  31.5 2.8 copy-start.13
  36.4 3.0 copy-start.10
  36.4 3.0 copy-start.14
  44.1 6.0 %copy-start.2 = (f32[641,6,160]{0,2,1:T(8,128)}, f32[641,6,160]{0,2,1:T(8,128)S(1)}, u32[]{:S(2)}) copy-start(f32[641,6,160]{0,2,1:T(8,128)S(1)} %get-tuple-element.111) | copy-start | bytes 7384324
  44.1 5.9 %copy-start.4 = (f32[641,6,160]{0,2,1:T(8,128)}, f32[641,6,160]{0,2,1:T(8,128)S(1)}, u32[]{:S(2)}) copy-start(f32[641,6,160]{0,2,1:T(8,128)S(1)} %get-tuple-element.112) | copy-start | bytes 7384324
  44.1 5.9 %copy-start.6 = (f32[641,6,160]{0,2,1:T(8,128)}, f32[641,6,160]{0,2,1:T(8,128)S(1)}, u32[]{:S(2)}) copy-start(f32[641,6,160]{0,2,1:T(8,128)S(1)} %get-tuple-element.110) | copy-start | bytes 7384324
  44.1 5.9 %copy-start.8 = (f32[641,6,160]{0,2,1:T(8,128)}, f32[641,6,160]{0,2,1:T(8,128)S(1)}, u32[]{:S(2)}) copy-start(f32[641,6,160]{0,2,1:T(8,128)S(1)} %get-tuple-element.113) | copy-start | bytes 7384324
  50.0 3.1 copy-start.21
  53.1 2.2 copy-start.16
  53.1 2.2 copy-start.11
  53.1 2.6 copy-start.22
  66.5 10.6 %all-to-all-start.1 = ((f32[8,2,1,72,1,20]{3,1,5,4,2,0:T(2,128)}), f32[8,2,1,72,1,20]{3,1,5,4,2,0:T(2,128)S(1)}, u32[]{:S(2)}, u32[]{:S(2)}) async-start(f32[8,2,1,72,1,20]{3,1,5,4,2,0:T(2,128)} %copy.71), calls=%async_computation.1 | async-start | bytes 327680 | tf_op jit(solution)/shard_map/all_to_all | solution.py:52
  71.5 391.3 %all-reduce.2.cloned.1.call-start = ((), (), s32[]{:S(2)}) async-start(), calls=%async_computation.4 | async-start | bytes 13656064 | tf_op jit(solution)/shard_map/psum | solution.py:68
  93.6 3.3 copy-start.17
  98.1 3.1 copy-start.19
  101.2 3.6 copy-start.12
  101.2 4.0 copy-start.9
  104.4 1.8 copy-start.7
  106.2 2.7 copy-start.5
  106.2 2.9 copy-start.15
  478.1 16.0 %copy-start.1 = (bf16[641,1282]{1,0:T(8,128)(2,1)S(1)}, bf16[641,1282]{1,0:T(8,128)(2,1)}, u32[]{:S(2)}) copy-start(bf16[641,1282]{1,0:T(8,128)(2,1)} %param.11) | copy-start | bytes 4930576
  (3 other events, 4.6 us)
Sparse Core Ops, SparseCore 0:
  182.7 280.0 all-reduce.1
where the time goes:
time: 508 us; the launch traced here: 502 us
  waiting for transfers between devices  248 us (49%)
  local copies, waits for them, and re-layouts  119 us (23%)
  blocking collectives  67.3 us (13%)
  other arithmetic  23.2 us (5%)
  between operations  16.4 us (3%)
  matrix products  15.7 us (3%)
  starting transfers between devices  12.5 us (2%)
    psum x1, waiting for transfers between devices, packed_total(): total = lax.psum(line, axis)  231 us
    concatenate x1, local copies, waits for them, and re-layouts, packed_total(): line, at, done = (jnp.concatenate([a.reshape(-1) for a in arrays]), 0, [])  59.2 us
    psum x5, blocking collectives, one_axis_at_a_time(): return functools.reduce(lax.psum, axes, shard)  47.7 us
    all_to_all x3, blocking collectives, moved_by_axis(): lax.all_to_all(pieces, axes[k], split_axis=k, concat_axis=k, tiled=True)  19.5 us
    reshape x4, local copies, waits for them, and re-layouts, packed_total(): done.append(total[at:at + a.size].reshape(a.shape))  14.3 us
    reshape x4, local copies, waits for them, and re-layouts, packed_total(): line, at, done = (jnp.concatenate([a.reshape(-1) for a in arrays]), 0, [])  11.3 us
    unnamed x49, local copies, waits for them, and re-layouts  10.9 us
    slice x4, local copies, waits for them, and re-layouts, packed_total(): done.append(total[at:at + a.size].reshape(a.shape))  10.7 us
  transfers between devices with their start and end apart: 4, of which 4 were waited for; matrix products, arithmetic and copies ran while one was open for 1% of the time, Pallas kernels for 0%

commit v1 on v0

--- a/solution.py
+++ b/solution.py
@@ -4,8 +4,333 @@
 import jax
 import jax.numpy as jnp
 from jax import lax
+from jax.experimental import pallas as pl
+from jax.experimental.pallas import tpu as pltpu
 from jax.sharding import Mesh
 from jax.sharding import PartitionSpec as P
+
+AXES = ("mem_0", "mem_1", "mem_2", "lat_0", "lat_1")
+MESH_ID = pl.DeviceIdType.MESH
+MAIN_ROWS, MAIN_COLS = 40, 10
+MAIN = MAIN_ROWS * MAIN_COLS
+SMALL_ROWS, SMALL_COLS = 4, 6
+UNITS = MAIN + SMALL_ROWS * SMALL_COLS
+PARTS = ((168, "xyz"), (168, "yxz"), (88, "zxy"))
+SIZE = {"x": 4, "y": 4, "z": 8}
+
+
+def place():
+    x = lax.axis_index("mem_0")
+    y = lax.axis_index("lat_0") * 2 + lax.axis_index("mem_1")
+    z = lax.axis_index("lat_1")
+    return {"x": x, "y": y, "z": z}
+
+
+def device_at(axis, p):
+    if axis == "x":
+        return {"mem_0": p}
+    if axis == "y":
+        return {"lat_0": p // 2, "mem_1": p % 2}
+    return {"lat_1": p}
+
+
+def steps_of():
+    plans, at = [], 0
+    for size, order in PARTS:
+        left, levels = size, []
+        for a in order:
+            left = -(-left // SIZE[a])
+            levels.append((a, SIZE[a], left))
+        plans.append((at, size, levels))
+        at += size
+    return plans
+
+
+def peers_of(at):
+    out = []
+    for a in "xyz":
+        for d in range(1, SIZE[a]):
+            out.append(device_at(a, (at[a] + d) % SIZE[a]))
+    return out
+
+
+def total_kernel(p_ref, loss_ref, g_ref, loss_out, *scratch):
+    plans = steps_of()
+    at = place()
+    core = lax.axis_index("mem_2")
+    sibling = {"mem_2": 1 - core}
+    it = iter(scratch)
+    core_in = next(it)
+    parts = []
+    for _ in plans:
+        parts.append([[next(it) for _ in range(4)] for _ in range(3)])
+    loss_in = next(it)
+    cs, cr, cs2, cr2 = next(it), next(it), next(it), next(it)
+    rs_s, rs_r, ag_s, ag_r = next(it), next(it), next(it), next(it)
+    ls, lr = next(it), next(it)
+
+    barrier = pltpu.get_barrier_semaphore()
+    everyone = [sibling] + peers_of(at)
+    for dev in everyone:
+        pl.semaphore_signal(barrier, inc=1, device_id=dev, device_id_type=MESH_ID)
+    pl.semaphore_wait(barrier, len(everyone))
+
+    def remote(src, dst, s, r, dev):
+        return pltpu.make_async_remote_copy(
+            src_ref=src, dst_ref=dst, send_sem=s, recv_sem=r, device_id=dev, device_id_type=MESH_ID
+        )
+
+    first = []
+    for k, (off, size, levels) in enumerate(plans):
+        c = remote(
+            p_ref.at[1 - core, pl.ds(off, size)], core_in.at[pl.ds(off, size)], cs.at[k], cr.at[k], sibling
+        )
+        c.start()
+        first.append(c)
+    open_copies = []
+    loss_steps = [("c", [sibling])] + [
+        (a, [device_at(a, (at[a] + d) % SIZE[a]) for d in range(1, SIZE[a])]) for a in "xyz"
+    ]
+    loss_value = loss_ref[...]
+
+    def loss_send(level, value):
+        base = (0, 2, 6, 10)[level]
+        sbase = (0, 1, 4, 7)[level]
+        loss_in[base] = value
+        started = []
+        for d, dev in enumerate(loss_steps[level][1]):
+            c = remote(loss_in.at[base], loss_in.at[base + 1 + d], ls.at[sbase + d], lr.at[sbase + d], dev)
+            c.start()
+            started.append(c)
+        return started
+
+    def loss_take(level, started):
+        base = (0, 2, 6, 10)[level]
+        for c in started:
+            c.wait()
+        total = loss_in[base]
+        for d in range(len(started)):
+            total = total + loss_in[base + 1 + d]
+        return total
+
+    loss_open = loss_send(0, loss_value)
+
+    running = [None] * len(plans)
+    for level in range(3):
+        for k, (off, size, levels) in enumerate(plans):
+            a, n, u = levels[level]
+            send, recv, total, gather = parts[k][level]
+            me = at[a]
+            if level == 0:
+                first[k].wait()
+                send[...] = (p_ref[core, off : off + size] + core_in[off : off + size]).astype(jnp.bfloat16)
+            else:
+                ua = levels[level - 1][1:]
+                prev_n, prev_u = ua
+                pa = levels[level - 1][0]
+                psend, precv, ptotal, _ = parts[k][level - 1]
+                for c in running[k]:
+                    c.wait_recv()
+                base = at[pa] * prev_u
+                if level == 1:
+                    value = p_ref[core, pl.ds(off + base, prev_u)] + core_in[pl.ds(off + base, prev_u)]
+                else:
+                    value = ptotal[pl.ds(base, prev_u)]
+                for d in range(prev_n - 1):
+                    value = value + precv[d].astype(jnp.float32)
+                total[0:prev_u] = value
+                if n * u > prev_u:
+                    total[prev_u:] = jnp.zeros((n * u - prev_u, 16, 128), jnp.float32)
+                send[...] = total[...].astype(jnp.bfloat16)
+            started = []
+            for d in range(1, n):
+                p = (me + d) % n
+                c = remote(
+                    send.at[pl.ds(p * u, u)],
+                    recv.at[d - 1],
+                    rs_s.at[k, level, d - 1],
+                    rs_r.at[k, level, d - 1],
+                    device_at(a, p),
+                )
+                c.start()
+                started.append(c)
+            running[k] = started
+            open_copies += started
+        loss_value = loss_take(level, loss_open)
+        loss_open = loss_send(level + 1, loss_value)
+
+    for level in (2, 1, 0):
+        for k, (off, size, levels) in enumerate(plans):
+            a, n, u = levels[level]
+            send, recv, total, gather = parts[k][level]
+            me = at[a]
+            target = g_ref.at[core] if level == 0 else gather
+            shift = off if level == 0 else 0
+            mine = pl.ds(shift + me * u, u)
+            if level == 2:
+                for c in running[k]:
+                    c.wait_recv()
+                value = total[pl.ds(me * u, u)]
+                for d in range(n - 1):
+                    value = value + recv[d].astype(jnp.float32)
+                target[mine] = value.astype(jnp.bfloat16)
+                source = target.at[mine]
+            else:
+                below = parts[k][level + 1][3]
+                for c in running[k]:
+                    c.wait_recv()
+                target[mine] = below[0:u]
+                source = below.at[pl.ds(0, u)]
+            started = []
+            for d in range(1, n):
+                c = remote(
+                    source,
+                    target.at[mine],
+                    ag_s.at[k, level, d - 1],
+                    ag_r.at[k, level, d - 1],
+                    device_at(a, (me + d) % n),
+                )
+                c.start()
+                started.append(c)
+            running[k] = started
+            open_copies += started
+            if level == 0:
+                c = remote(
+                    g_ref.at[core, mine], g_ref.at[core, mine], cs2.at[k, 0], cr2.at[k, 0], sibling
+                )
+                c.start()
+                open_copies.append(c)
+                running[k] = (started, [c])
+    loss_out[...] = loss_take(3, loss_open)
+    last = []
+    for d in range(1, 4):
+        for k, (off, size, levels) in enumerate(plans):
+            a, n, u = levels[0]
+            for dd in range(d, d + 1) if d < 3 else range(3, n):
+                if dd >= n:
+                    continue
+                started, sent = running[k]
+                started[dd - 1].wait_recv()
+                src = (at[a] + n - dd) % n
+                piece = pl.ds(off + src * u, u)
+                c = remote(g_ref.at[core, piece], g_ref.at[core, piece], cs2.at[k, dd], cr2.at[k, dd], sibling)
+                c.start()
+                sent.append(c)
+                open_copies.append(c)
+    for k in range(len(plans)):
+        for c in running[k][1]:
+            c.wait_recv()
+    for c in open_copies:
+        c.wait_send()
+
+
+def total_of(partial, loss):
+    plans = steps_of()
+    scratch = [pltpu.VMEM((UNITS, 16, 128), jnp.float32)]
+    for off, size, levels in plans:
+        for a, n, u in levels:
+            scratch += [
+                pltpu.VMEM((n * u, 16, 128), jnp.bfloat16),
+                pltpu.VMEM((n - 1, u, 16, 128), jnp.bfloat16),
+                pltpu.VMEM((n * u, 16, 128), jnp.float32),
+                pltpu.VMEM((n * u, 16, 128), jnp.bfloat16),
+            ]
+    scratch += [
+        pltpu.VMEM((18, 8, 128), jnp.float32),
+        pltpu.SemaphoreType.DMA((3,)),
+        pltpu.SemaphoreType.DMA((3,)),
+        pltpu.SemaphoreType.DMA((3, 8)),
+        pltpu.SemaphoreType.DMA((3, 8)),
+        pltpu.SemaphoreType.DMA((3, 3, 7)),
+        pltpu.SemaphoreType.DMA((3, 3, 7)),
+        pltpu.SemaphoreType.DMA((3, 3, 7)),
+        pltpu.SemaphoreType.DMA((3, 3, 7)),
+        pltpu.SemaphoreType.DMA((14,)),
+        pltpu.SemaphoreType.DMA((14,)),
+    ]
+    vmem = pl.BlockSpec(memory_space=pltpu.VMEM)
+    return pl.pallas_call(
+        total_kernel,
+        out_shape=(
+            jax.ShapeDtypeStruct((2, UNITS, 16, 128), jnp.bfloat16),
+            jax.ShapeDtypeStruct((8, 128), jnp.float32),
+        ),
+        in_specs=[vmem, vmem],
+        out_specs=(vmem, vmem),
+        scratch_shapes=scratch,
+        compiler_params=pltpu.CompilerParams(
+            collective_id=0, has_side_effects=True, vmem_limit_bytes=48 * 1024 * 1024
+        ),
+    )(partial, loss)
+
+
+def unpack_kernel(g_ref, up_ref, down_ref, head_ref, kern_ref, gain_ref, small):
+    for m, out in enumerate((up_ref, down_ref)):
+        for j in range(MAIN_COLS):
+            piece = g_ref[m, pl.ds(j, MAIN_ROWS, stride=MAIN_COLS)].astype(jnp.float32)
+            out[0:640, j * 128 : (j + 1) * 128] = piece.reshape(640, 128)
+        for j in range(SMALL_COLS):
+            piece = g_ref[m, pl.ds(MAIN + j, SMALL_ROWS, stride=SMALL_COLS)].astype(jnp.float32)
+            small[m, :, j * 128 : (j + 1) * 128] = piece.reshape(64, 128)
+    head_ref[0:64, :] = small[0, :, 0:641]
+    head_ref[64:72, :] = small[1, 0:8, 0:641]
+    kern_ref[...] = small[1, 8:33, 0:641]
+    gain_ref[...] = small[1, 33:34, 0:641]
+    for m, out in enumerate((up_ref, down_ref)):
+        r = 34 + 5 * m
+        edge = small[1, 32:56, :]
+        cols = jnp.transpose(edge)[0:641, r - 32 : r - 30]
+        out[:, 1280:1282] = cols
+        out[640:641, 0:640] = small[1, r + 2 : r + 3, 0:640]
+        out[640:641, 640:1280] = small[1, r + 3 : r + 4, 0:640]
+        out[640:641, 1280:1282] = small[1, r + 4 : r + 5, 0:2]
+
+
+def unpacked(g):
+    vmem = pl.BlockSpec(memory_space=pltpu.VMEM)
+    f32 = jnp.float32
+    return pl.pallas_call(
+        unpack_kernel,
+        out_shape=(
+            jax.ShapeDtypeStruct((641, 1282), f32),
+            jax.ShapeDtypeStruct((641, 1282), f32),
+            jax.ShapeDtypeStruct((72, 641), f32),
+            jax.ShapeDtypeStruct((25, 641), f32),
+            jax.ShapeDtypeStruct((1, 641), f32),
+        ),
+        in_specs=[vmem],
+        out_specs=(vmem,) * 5,
+        scratch_shapes=[pltpu.VMEM((2, 64, 768), f32)],
+        compiler_params=pltpu.CompilerParams(vmem_limit_bytes=48 * 1024 * 1024),
+    )(g)
+
+
+def packed(grad_kernel, grad_gain, grad_up, grad_down_t, grad_head_t):
+    def main(g):
+        return g[:640, :1280].reshape(40, 16, 10, 128).transpose(0, 2, 1, 3).reshape(400, 16, 128)
+
+    def rows(a):
+        return jnp.pad(a, ((0, 0), (0, 768 - a.shape[1])))
+
+    def edges(g):
+        return [
+            rows(g[:, 1280:1282].T),
+            rows(g[640:641, 0:640]),
+            rows(g[640:641, 640:1280]),
+            rows(g[640:641, 1280:1282]),
+        ]
+
+    def small(pieces):
+        s = jnp.concatenate(pieces, axis=0)
+        s = jnp.pad(s, ((0, 64 - s.shape[0]), (0, 0)))
+        return s.reshape(4, 16, 6, 128).transpose(0, 2, 1, 3).reshape(24, 16, 128)
+
+    s0 = small([rows(grad_head_t[:64])])
+    s1 = small([rows(grad_head_t[64:]), rows(grad_kernel), rows(grad_gain[None])] + edges(grad_up) + edges(grad_down_t))
+    return jnp.stack(
+        [jnp.concatenate([main(grad_up), s0]), jnp.concatenate([main(grad_down_t), s1])]
+    )
+
 
 MEM = ("mem_0", "mem_1", "mem_2")
 LAT = ("lat_0", "lat_1")
@@ -57,19 +382,6 @@
     count = lax.axis_size(groups[0]) * lax.axis_size(groups[1])
     pieces = cut_along(shard, split_dim, count)
     return joined_along(moved_by_axis(pieces, groups, sequence), concat_dim)
-
-
-def one_axis_at_a_time(shard, axes):
-    return functools.reduce(lax.psum, axes, shard)
-
-
-def packed_total(arrays, axis):
-    line, at, done = (jnp.concatenate([a.reshape(-1) for a in arrays]), 0, [])
-    total = lax.psum(line, axis)
-    for a in arrays:
-        done.append(total[at : at + a.size].reshape(a.shape))
-        at += a.size
-    return tuple(done)
 
 
 def softened_absolute(diff):
@@ -219,7 +531,6 @@
         - jnp.sum(softened_absolute(differences), axis=(0, 1)) / pair_norm
     )
     partial_value = jnp.sum(field_weight[:, None] * area_block[None, :] * ensemble_spread)
-    loss = one_axis_at_a_time(partial_value, MEM_LAT) / member_count
     pairwise_derivatives = jnp.sum(softened_derivative(differences), axis=1)
     member_cot = (
         field_weight[None, :, None]
@@ -236,8 +547,11 @@
     grads = backward(
         window, stored_residuals, cotangent, norm_gain, up_weight, down_weight, field_head_weight
     )
-    totals = packed_total((grads[0], grads[1], grads[2], grads[3], grads[4]), MEM_LAT)
-    return (loss, totals[0], totals[1], totals[2], totals[3], totals[4])
+    grads_t = (grads[0], grads[1], grads[2], grads[3].T, grads[4].T)
+    loss_tile = jnp.full((8, 128), partial_value / member_count, jnp.float32)
+    total, loss_total = total_of(packed(*grads_t), loss_tile)
+    up, down_t, head_t, kern, gain_row = unpacked(total)
+    return (loss_total[0, 0], kern, gain_row[0], up, down_t.T, head_t.T)
 
 
 def solution(mesh):

time: 508 us -> 207 us (0.41)
  waiting for transfers between devices: 248 us -> 20.1 us
  local copies, waits for them, and re-layouts: 119 us -> 44.6 us
  Pallas kernels: 0 us -> 70.3 us
  blocking collectives: 67.3 us -> 12 us
  between operations: 16.4 us -> 2.06 us
    psum x1 -> x0, waiting for transfers between devices: 231 us -> none  [packed_total(): total = lax.psum(line, axis)]
    pallas_call x0 -> x2, Pallas kernels: none -> 70.3 us  [the longest x1 66.8 us: total_of(): pl.pallas_call(total_kernel, out_shape=(jax.ShapeDtypeStruct((2, UNITS, 1...]
    concatenate x1, local copies, waits for them, and re-layouts: 59.2 us -> 0.2 us  [small(): s = jnp.concatenate(pieces, axis=0)]
    psum x5 -> x0, blocking collectives: 47.7 us -> none  [one_axis_at_a_time(): return functools.reduce(lax.psum, axes, shard)]
    reshape x8 -> x4, local copies, waits for them, and re-layouts: 25.6 us -> 9.89 us  [the longest x2 9.82 us: main(): g[:640, :1280].reshape(40, 16, 10, 128).transpose(0, 2, 1, 3)]
    transpose x0 -> x6, local copies, waits for them, and re-layouts: none -> 9.85 us  [the longest x2 9.72 us: main(): g[:640, :1280].reshape(40, 16, 10, 128).transpose(0, 2, 1, 3)]
    all_to_all x3 -> x2, blocking collectives: 19.5 us -> 12 us  [moved_by_axis(): lax.all_to_all(pieces, axes[k], split_axis=k, concat_axis=k, tiled=True)]
    slice x4 -> x11, local copies, waits for them, and re-layouts: 10.7 us -> 4.45 us  [the longest x2 3.91 us: main(): g[:640, :1280].reshape(40, 16, 10, 128).transpose(0, 2, 1, 3)]
  transfers between devices with their start and end apart: 4 -> 4, of which waited for: 4 -> 4; matrix products, arithmetic and copies ran while one was open for 1% -> 4% of each run, Pallas kernels for 0% -> 0%
where the time goes in v1:
time: 207 us; the launch traced here: 206 us
  Pallas kernels  70.3 us (34%)
  local copies, waits for them, and re-layouts  44.6 us (22%)
  other arithmetic  27.7 us (13%)
  waiting for transfers between devices  20.1 us (10%)
  starting transfers between devices  16 us (8%)
  matrix products  12.9 us (6%)
  blocking collectives  12 us (6%)
    pallas_call x1, Pallas kernels, total_of(): pl.pallas_call(total_kernel, out_shape=(jax.ShapeDtypeStruct((2, UNITS, 1...  66.8 us
    all_to_all x2, blocking collectives, moved_by_axis(): lax.all_to_all(pieces, axes[k], split_axis=k, concat_axis=k, tiled=True)  12 us
    ppermute x1, waiting for transfers between devices, extended(): lax.ppermute(head, axis, [((i + 1) % count, i) for i in range(ends)])  10.6 us
    reshape x2, local copies, waits for them, and re-layouts, main(): g[:640, :1280].reshape(40, 16, 10, 128).transpose(0, 2, 1, 3)  9.82 us
    transpose x2, local copies, waits for them, and re-layouts, main(): g[:640, :1280].reshape(40, 16, 10, 128).transpose(0, 2, 1, 3)  9.72 us
    all_to_all x2, starting transfers between devices, moved_by_axis(): lax.all_to_all(pieces, axes[k], split_axis=k, concat_axis=k, tiled=True)  8.57 us
    all_to_all x2, waiting for transfers between devices, moved_by_axis(): lax.all_to_all(pieces, axes[k], split_axis=k, concat_axis=k, tiled=True)  8.52 us
    ppermute x1, starting transfers between devices, extended(): lax.ppermute(tail, axis, [(i, (i + 1) % count) for i in range(ends)])  5.99 us
  transfers between devices with their start and end apart: 4, of which 4 were waited for; matrix products, arithmetic and copies ran while one was open for 4% of the time, Pallas kernels for 0%

profile of v1, /device:TPU:1, one launch (start us, length us, event | category | flops | bytes accessed | tf_op | source)
XLA Modules:
  0.0 205.6 jit_solution(5694168901479778824)
XLA Ops:
  2.1 6.0 %collective-permute-start = (f32[641,2,160]{0,2,1:T(8,128)}, f32[641,2,160]{0,2,1:T(8,128)}, u32[]{:S(2)}, u32[]{:S(2)}) collective-permute-start(f32[641,2,160]{0,2,1:T(8,128)} %bitcast.83), channel_id=1, source_target_pairs={{0,1},{1,2},{2,3},{3,4},{4,5},{5,6},{6,7},{7,8},{8,9},{9,10},{10,1... | collective-permute-start | bytes 2461448 | tf_op jit(solution)/shard_map/ppermute | solution.py:352
  14.3 10.6 %collective-permute-done.1 = f32[641,2,160]{0,2,1:T(8,128)S(1)} collective-permute-done((f32[641,2,160]{0,2,1:T(8,128)}, f32[641,2,160]{0,2,1:T(8,128)S(1)}, u32[]{:S(2)}, u32[]{:S(2)}) %collective-permute-start.1) | collective-permute-done | bytes 820512 | tf_op jit(solution)/shard_map/ppermute | solution.py:354
  27.8 2.1 %fusion.29 = (f32[641,6,158]{0,2,1:T(8,128)S(1)}, f32[641,6,158]{0,2,1:T(8,128)}) fusion(f32[641,6,160]{0,2,1:T(8,128)S(1)} %pad_maximum_fusion.9), kind=kLoop, calls=%fused_computation.127 | loop fusion | bytes 9722688 | tf_op jit(solution)/shard_map/jit(_roll_static)/slice | solution.py:416
  29.9 3.0 %fusion.30 = (f32[641,6,159]{0,2,1:T(8,128)}, f32[641,6,159]{0,2,1:T(8,128)}) fusion(f32[641,6,160]{0,2,1:T(8,128)S(1)} %pad_maximum_fusion.9), kind=kLoop, calls=%fused_computation.128 | loop fusion | bytes 9784224 | tf_op jit(solution)/shard_map/jit(_roll_static)/slice | solution.py:416
  32.9 4.6 %fusion.3 = (f32[641,6,160]{0,2,1:T(8,128)S(1)}, f32[641,6,160]{0,2,1:T(8,128)S(1)}, f32[641,6,160]{0,2,1:T(8,128)S(1)}, f32[641,6,160]{0,2,1:T(8,128)S(1)}) fusion(f32[641,2,160]{0,2,1:T(8,128)S(1)} %copy-done.14, f32[641,2,160]{0,2,1:T(8,128)S(1)} %bitcast.85, f32[641,2,160]{0,2,1:T(8,128)} %collective-permute-done, ...), kind=kLoop, calls=%fused_computation.15 | loop fusion | flops 7384320 | bytes 22060656 | tf_op jit(solution)/shard_map/jit(_roll_static)/concatenate | solution.py:416
  37.6 5.9 %fusion.26 = (f32[2,160]{1,0:T(2,128)S(1)}, f32[641,2,160]{0,2,1:T(8,128)}) fusion(f32[641,2,160]{0,2,1:T(8,128)S(1)} %bitcast.86, f32[641,6,160]{0,2,1:T(8,128)S(1)} %get-tuple-element.98, f32[641]{0:T(1024)S(1)} %get-tuple-element.86, f32[641]{0:T(1024)S(1)} %get-tuple-element.87, f32[641]{0:T(1024)S(1)} %get-tuple-element.64, ...), kind=kLoop, calls=%fused_computation.124 | loop fusion | flops 10871040 | bytes 19756900 | tf_op jit(solution)/shard_map/reduce_sum | solution.py:441
  46.6 2.2 %multiply_convert_fusion = (bf16[1282,320]{0,1:T(8,128)(2,1)S(1)}, f32[1282,320]{0,1:T(8,128)}) fusion(bf16[641,1282]{1,0:T(8,128)(2,1)S(1)} %copy-done, f32[641,320]{0,1:T(8,128)S(1)} %fusion.18, f32[641]{0:T(1024)S(1)} %copy-done.23), kind=kOutput, calls=%fused_computation.32 | convolution fusion | flops 528389120 | bytes 4928008 | tf_op jit(solution)/shard_map/dot_general | solution.py:402
  52.3 6.9 %all_to_all.20 = f32[8,2,1,72,1,20]{3,0,5,4,2,1:T(8,128)S(1)} all-to-all(f32[8,2,1,72,1,20]{3,0,5,4,2,1:T(8,128)S(1)} %copy.83), channel_id=1, replica_groups=mesh['mem_0'=4,'mem_1'=2,'mem_2'=2,'lat_0'=2,'lat_1'=8] {'mem_2'}, dimensions={1} | all-to-all | bytes 184320 | tf_op jit(solution)/shard_map/all_to_all | solution.py:377
  60.0 5.0 %all-to-all-start.1 = ((f32[8,2,1,72,1,20]{3,1,5,4,2,0:T(2,128)}), f32[8,2,1,72,1,20]{3,1,5,4,2,0:T(2,128)S(1)}, u32[]{:S(2)}, u32[]{:S(2)}) async-start(f32[8,2,1,72,1,20]{3,1,5,4,2,0:T(2,128)} %copy.84), calls=%async_computation.1 | async-start | bytes 327680 | tf_op jit(solution)/shard_map/all_to_all | solution.py:377
  65.8 4.9 %all-to-all-done.1 = f32[8,2,1,72,1,20]{3,1,5,4,2,0:T(2,128)S(1)} async-done(((f32[8,2,1,72,1,20]{3,1,5,4,2,0:T(2,128)}), f32[8,2,1,72,1,20]{3,1,5,4,2,0:T(2,128)S(1)}, u32[]{:S(2)}, u32[]{:S(2)}) %all-to-all-start.1) | async-done | bytes 92192 | tf_op jit(solution)/shard_map/all_to_all | solution.py:377
  70.8 2.2 %fusion.10 = (f32[72,20]{0,1:T(8,128)S(1)}, f32[16,72,20]{1,2,0:T(8,128)S(1)}) fusion(f32[16,72,20]{1,0,2:T(8,128)S(1)} %bitcast.102, f32[16,72,20]{1,2,0:T(8,128)S(1)} %copy.88), kind=kLoop, calls=%fused_computation.27 | loop fusion | flops 2556000 | bytes 282240 | tf_op jit(solution)/shard_map/reduce_sum | solution.py:531
  73.2 5.1 %all_to_all.21 = bf16[8,2,1,72,1,20]{3,0,5,4,2,1:T(8,128)(2,1)S(1)} all-to-all(bf16[8,2,1,72,1,20]{3,0,5,4,2,1:T(8,128)(2,1)S(1)} %get-tuple-element.105), channel_id=1, replica_groups=mesh['mem_0'=4,'mem_1'=2,'mem_2'=2,'lat_0'=2,'lat_1'=8] {'mem_2'}, dimensions={1} | all-to-all | bytes 92160 | tf_op jit(solution)/shard_map/all_to_all | solution.py:377
  79.0 3.5 %all-to-all-start.3 = ((bf16[8,2,1,72,1,20]{3,1,5,4,2,0:T(2,128)(2,1)}), bf16[8,2,1,72,1,20]{3,1,5,4,2,0:T(2,128)(2,1)S(1)}, u32[]{:S(2)}, u32[]{:S(2)}) async-start(bf16[8,2,1,72,1,20]{3,1,5,4,2,0:T(2,128)(2,1)} %copy.91), calls=%async_computation.3 | async-start | bytes 163840 | tf_op jit(solution)/shard_map/all_to_all | solution.py:377
  83.8 3.6 %all-to-all-done.3 = bf16[8,2,1,72,1,20]{3,1,5,4,2,0:T(2,128)(2,1)S(1)} async-done(((bf16[8,2,1,72,1,20]{3,1,5,4,2,0:T(2,128)(2,1)}), bf16[8,2,1,72,1,20]{3,1,5,4,2,0:T(2,128)(2,1)S(1)}, u32[]{:S(2)}, u32[]{:S(2)}) %all-to-all-start.3) | async-done | bytes 46112 | tf_op jit(solution)/shard_map/all_to_all | solution.py:377
  90.6 3.3 %fusion.5 = bf16[1282,320]{0,1:T(8,128)(2,1)S(1)} fusion(bf16[1282,641]{0,1:T(8,128)(2,1)} %param.12, f32[1282,320]{0,1:T(8,128)} %get-tuple-element.107, f32[641,320]{0,1:T(8,128)S(1)} %convolution_bitcast_fusion.3), kind=kOutput, calls=%fused_computation.22 | convolution fusion | flops 530235200 | bytes 4925444 | tf_op jit(solution)/shard_map/dot_general | solution.py:478
  97.7 2.0 slice.344
  106.9 2.5 %multiply_reduce_fusion.1 = (f32[641]{0:T(1024)S(1)}, f32[641]{0:T(1024)S(1)}, f32[641]{0:T(1024)S(1)}, f32[641]{0:T(1024)S(1)}, f32[641]{0:T(1024)S(1)}, /*inde...) fusion(f32[641,2,160]{0,2,1:T(8,128)S(1)} %bitcast.94, ...), kind=kLoop, calls=%fused_computation.47 | loop fusion | flops 6144626 | bytes 11522616 | tf_op jit(solution)/shard_map/reduce_sum | solution.py:431
  110.7 4.9 %reshape.153 = f32[40,16,10,128]{3,2,1,0:T(8,128)} reshape(f32[640,1280]{1,0:T(8,128)} %slice.344) | data formatting | bytes 6553600 | tf_op jit(solution)/shard_map/reshape | solution.py:310
  115.6 5.7 %copy.96 = f32[40,10,16,128]{3,2,1,0:T(8,128)} copy(f32[40,10,16,128]{3,1,2,0:T(8,128)} %bitcast.88) | data formatting | bytes 6553600 | tf_op jit(solution)/shard_map/transpose | solution.py:310
  121.4 4.9 %reshape.149 = f32[40,16,10,128]{3,2,1,0:T(8,128)} reshape(f32[640,1280]{1,0:T(8,128)} %slice.342) | data formatting | bytes 6553600 | tf_op jit(solution)/shard_map/reshape | solution.py:310
  126.3 4.1 %copy.94 = f32[40,10,16,128]{3,2,1,0:T(8,128)S(1)} copy(f32[40,10,16,128]{3,1,2,0:T(8,128)} %bitcast.89) | data formatting | bytes 6553600 | tf_op jit(solution)/shard_map/transpose | solution.py:310
  130.8 3.3 %pad_maximum_fusion.p_ref = f32[2,424,16,128]{3,2,1,0:T(8,128)} fusion(f32[1,424,16,128]{3,2,1,0:T(8,128)S(1)} %maximum_bitcast_fusion.1, f32[1,424,16,128]{3,2,1,0:T(8,128)S(1)} %maximum_bitcast_fusion), kind=kLoop, calls=%fused_computation | loop fusion | flops 1736704 | bytes 13893632 | tf_op jit(solution)/shard_map/stack | solution.py:330
  134.1 66.8 %shard_map.127 = (bf16[2,424,16,128]{3,2,1,0:T(8,128)(2,1)S(1)}, f32[8,128]{1,0:T(8,128)S(1)}) custom-call(f32[2,424,16,128]{3,2,1,0:T(8,128)} %pad_maximum_fusion.p_ref, f32[8,128]{1,0:T(8,128)S(1)} %broadcast_in_dim.11.loss_ref), custom_call_target="tpu_custom_call" | custom-call | tf_op jit(solution)/shard_map/pallas_call | solution.py:252
  201.5 3.5 %shard_map.128 = (f32[641,1282]{1,0:T(8,128)}, f32[641,1282]{1,0:T(8,128)}, f32[72,641]{1,0:T(8,128)}, f32[25,641]{1,0:T(8,128)}, f32[1,641]{1,0:T(1,128)S(1)}) custom-call(bf16[2,424,16,128]{3,2,1,0:T(8,128)(2,1)S(1)} %get-tuple-element.14.g_ref), custom_call_target="tpu_custom_call" | custom-call | tf_op jit(solution)/shard_map/pallas_call | solution.py:292
  (155 shorter events, 36.8 us)
Async XLA Ops:
  0.6 46.0 %copy-start = (bf16[641,1282]{1,0:T(8,128)(2,1)S(1)}, bf16[641,1282]{1,0:T(8,128)(2,1)}, u32[]{:S(2)}) copy-start(bf16[641,1282]{1,0:T(8,128)(2,1)} %param.11) | copy-start | bytes 4930576
  0.6 24.3 %collective-permute-start.1 = (f32[641,2,160]{0,2,1:T(8,128)}, f32[641,2,160]{0,2,1:T(8,128)S(1)}, u32[]{:S(2)}, u32[]{:S(2)}) collective-permute-start(f32[641,2,160]{0,2,1:T(8,128)} %bitcast.82), channel_id=1, source_target_pairs={{1,0},{2,1},{3,2},{4,3},{5,4},{6,5},{7,6},{8,7},{9,8},{10,9},{11,1... | collective-permute-start | bytes 2461448 | tf_op jit(solution)/shard_map/ppermute | solution.py:354
  2.1 23.9 %collective-permute-start = (f32[641,2,160]{0,2,1:T(8,128)}, f32[641,2,160]{0,2,1:T(8,128)}, u32[]{:S(2)}, u32[]{:S(2)}) collective-permute-start(f32[641,2,160]{0,2,1:T(8,128)} %bitcast.83), channel_id=1, source_target_pairs={{0,1},{1,2},{2,3},{3,4},{4,5},{5,6},{6,7},{7,8},{8,9},{9,10},{10,1... | collective-permute-start | bytes 2461448 | tf_op jit(solution)/shard_map/ppermute | solution.py:352
  24.9 2.8 %copy-start.13 = (f32[641,2,160]{0,2,1:T(8,128)}, f32[641,2,160]{0,2,1:T(8,128)S(1)}, u32[]{:S(2)}) copy-start(f32[641,2,160]{0,2,1:T(8,128)S(1)} %collective-permute-done.1) | copy-start | bytes 2461444
  29.9 3.0 %copy-start.10 = (f32[1,641,2,160]{1,3,2,0:T(8,128)S(1)}, f32[1,641,2,160]{1,3,2,0:T(8,128)}, u32[]{:S(2)}) copy-start(f32[1,641,2,160]{1,3,2,0:T(8,128)} %param.8) | copy-start | bytes 2461444
  29.9 3.0 %copy-start.14 = (f32[641,2,160]{0,2,1:T(8,128)S(1)}, f32[641,2,160]{0,2,1:T(8,128)}, u32[]{:S(2)}) copy-start(f32[641,2,160]{0,2,1:T(8,128)} %copy-done.13) | copy-start | bytes 2461444
  37.5 6.0 %copy-start.2 = (f32[641,6,160]{0,2,1:T(8,128)}, f32[641,6,160]{0,2,1:T(8,128)S(1)}, u32[]{:S(2)}) copy-start(f32[641,6,160]{0,2,1:T(8,128)S(1)} %get-tuple-element.97) | copy-start | bytes 7384324
  37.5 6.0 %copy-start.4 = (f32[641,6,160]{0,2,1:T(8,128)}, f32[641,6,160]{0,2,1:T(8,128)S(1)}, u32[]{:S(2)}) copy-start(f32[641,6,160]{0,2,1:T(8,128)S(1)} %get-tuple-element.98) | copy-start | bytes 7384324
  37.6 6.0 %copy-start.6 = (f32[641,6,160]{0,2,1:T(8,128)}, f32[641,6,160]{0,2,1:T(8,128)S(1)}, u32[]{:S(2)}) copy-start(f32[641,6,160]{0,2,1:T(8,128)S(1)} %get-tuple-element.96) | copy-start | bytes 7384324
  37.6 6.0 %copy-start.8 = (f32[641,6,160]{0,2,1:T(8,128)}, f32[641,6,160]{0,2,1:T(8,128)S(1)}, u32[]{:S(2)}) copy-start(f32[641,6,160]{0,2,1:T(8,128)S(1)} %get-tuple-element.99) | copy-start | bytes 7384324
  43.5 3.1 %copy-start.23 = (f32[641]{0:T(1024)S(1)}, f32[641]{0:T(1024)}, u32[]{:S(2)}) copy-start(f32[641]{0:T(1024)} %param.10) | copy-start | bytes 7696
  46.6 2.6 %copy-start.24 = (bf16[1282,641]{0,1:T(8,128)(2,1)S(1)}, bf16[1282,641]{0,1:T(8,128)(2,1)}, u32[]{:S(2)}) copy-start(bf16[1282,641]{0,1:T(8,128)(2,1)} %param.12) | copy-start | bytes 4930576
  60.0 10.6 %all-to-all-start.1 = ((f32[8,2,1,72,1,20]{3,1,5,4,2,0:T(2,128)}), f32[8,2,1,72,1,20]{3,1,5,4,2,0:T(2,128)S(1)}, u32[]{:S(2)}, u32[]{:S(2)}) async-start(f32[8,2,1,72,1,20]{3,1,5,4,2,0:T(2,128)} %copy.84), calls=%async_computation.1 | async-start | bytes 327680 | tf_op jit(solution)/shard_map/all_to_all | solution.py:377
  79.0 8.4 %all-to-all-start.3 = ((bf16[8,2,1,72,1,20]{3,1,5,4,2,0:T(2,128)(2,1)}), bf16[8,2,1,72,1,20]{3,1,5,4,2,0:T(2,128)(2,1)S(1)}, u32[]{:S(2)}, u32[]{:S(2)}) async-start(bf16[8,2,1,72,1,20]{3,1,5,4,2,0:T(2,128)(2,1)} %copy.91), calls=%async_computation.3 | async-start | bytes 163840 | tf_op jit(solution)/shard_map/all_to_all | solution.py:377
  89.3 10.4 %copy-start.21 = (f32[72,641]{1,0:T(8,128)}, f32[72,641]{1,0:T(8,128)S(1)}, u32[]{:S(2)}) copy-start(f32[72,641]{1,0:T(8,128)S(1)} %fusion.31) | copy-start | bytes 553828
  90.6 3.3 %copy-start.18 = (f32[641,320]{0,1:T(8,128)S(1)}, f32[641,320]{0,1:T(8,128)}, u32[]{:S(2)}) copy-start(f32[641,320]{0,1:T(8,128)} %copy-done.17) | copy-start | bytes 2461444
  99.7 3.3 %copy-start.9 = (f32[641,6,160]{0,2,1:T(8,128)S(1)}, f32[641,6,160]{0,2,1:T(8,128)}, u32[]{:S(2)}) copy-start(f32[641,6,160]{0,2,1:T(8,128)} %copy-done.8) | copy-start | bytes 7384324
  101.6 2.4 %copy-start.7 = (f32[641,6,160]{0,2,1:T(8,128)S(1)}, f32[641,6,160]{0,2,1:T(8,128)}, u32[]{:S(2)}) copy-start(f32[641,6,160]{0,2,1:T(8,128)} %copy-done.6) | copy-start | bytes 7384324
  104.0 2.7 %copy-start.5 = (f32[641,6,160]{0,2,1:T(8,128)S(1)}, f32[641,6,160]{0,2,1:T(8,128)}, u32[]{:S(2)}) copy-start(f32[641,6,160]{0,2,1:T(8,128)} %copy-done.4) | copy-start | bytes 7384324
  104.0 2.9 %copy-start.15 = (f32[641,2,160]{0,2,1:T(8,128)S(1)}, f32[641,2,160]{0,2,1:T(8,128)}, u32[]{:S(2)}) copy-start(f32[641,2,160]{0,2,1:T(8,128)} %copy-done.13) | copy-start | bytes 2461444
  106.9 2.8 %slice-start = ((f32[72,641]{1,0:T(8,128)}), f32[8,641]{1,0:T(8,128)S(1)}, s32[]{:S(2)}) async-start(f32[72,641]{1,0:T(8,128)} %copy-done.21), calls=%async_computation.4 | async-start | bytes 49152 | tf_op jit(solution)/shard_map/slice | solution.py:329
  115.6 5.7 %slice-start.1 = ((f32[72,641]{1,0:T(8,128)}), f32[64,641]{1,0:T(8,128)S(1)}, s32[]{:S(2)}) async-start(f32[72,641]{1,0:T(8,128)} %copy-done.21), calls=%async_computation.5 | async-start | bytes 393216 | tf_op jit(solution)/shard_map/slice | solution.py:328
  126.3 4.1 %copy-start.16 = (f32[40,10,16,128]{3,2,1,0:T(8,128)S(1)}, f32[40,10,16,128]{3,2,1,0:T(8,128)}, u32[]{:S(2)}) copy-start(f32[40,10,16,128]{3,2,1,0:T(8,128)} %copy.96) | copy-start | bytes 9830404
  134.1 71.5 %copy-start.1 = (bf16[641,1282]{1,0:T(8,128)(2,1)S(1)}, bf16[641,1282]{1,0:T(8,128)(2,1)}, u32[]{:S(2)}) copy-start(bf16[641,1282]{1,0:T(8,128)(2,1)} %param.11) | copy-start | bytes 4930576
  (7 other events, 12.3 us)

commit v2 on v1

v2 whole, which is shorter than its diff:
```python
import functools
import math

import jax
import jax.numpy as jnp
import numpy as np
from jax import lax
from jax.experimental import pallas as pl
from jax.experimental.pallas import tpu as pltpu
from jax.sharding import Mesh
from jax.sharding import PartitionSpec as P

AXES = ("mem_0", "mem_1", "mem_2", "lat_0", "lat_1")
MESH_ID = pl.DeviceIdType.MESH
MAIN_ROWS, MAIN_COLS = 40, 10
MAIN = MAIN_ROWS * MAIN_COLS
SMALL_ROWS, SMALL_COLS = 4, 6
UNITS = MAIN + SMALL_ROWS * SMALL_COLS
PARTS = ((168, "xyz"), (168, "yxz"), (88, "zxy"))
SIZE = {"x": 4, "y": 4, "z": 8}


def place():
    x = lax.axis_index("mem_0")
    y = lax.axis_index("lat_0") * 2 + lax.axis_index("mem_1")
    z = lax.axis_index("lat_1")
    return {"x": x, "y": y, "z": z}


def device_at(axis, p):
    if axis == "x":
        return {"mem_0": p}
    if axis == "y":
        return {"lat_0": p // 2, "mem_1": p % 2}
    return {"lat_1": p}


def steps_of():
    plans, at = [], 0
    for size, order in PARTS:
        left, levels = size, []
        for a in order:
            left = -(-left // SIZE[a])
            levels.append((a, SIZE[a], left))
        plans.append((at, size, levels))
        at += size
    return plans


def peers_of(at):
    out = []
    for a in "xyz":
        for d in range(1, SIZE[a]):
            out.append(device_at(a, (at[a] + d) % SIZE[a]))
    return out


def total_kernel(p_ref, loss_ref, g_ref, loss_out, *scratch):
    plans = steps_of()
    at = place()
    core = lax.axis_index("mem_2")
    sibling = {"mem_2": 1 - core}
    it = iter(scratch)
    core_in = next(it)
    parts = []
    for _ in plans:
        parts.append([[next(it) for _ in range(4)] for _ in range(3)])
    loss_in = next(it)
    cs, cr, cs2, cr2 = next(it), next(it), next(it), next(it)
    rs_s, rs_r, ag_s, ag_r = next(it), next(it), next(it), next(it)
    ls, lr = next(it), next(it)

    barrier = pltpu.get_barrier_semaphore()
    everyone = [sibling] + peers_of(at)
    for dev in everyone:
        pl.semaphore_signal(barrier, inc=1, device_id=dev, device_id_type=MESH_ID)
    pl.semaphore_wait(barrier, len(everyone))

    def remote(src, dst, s, r, dev):
        return pltpu.make_async_remote_copy(
            src_ref=src, dst_ref=dst, send_sem=s, recv_sem=r, device_id=dev, device_id_type=MESH_ID
        )

    first = []
    for k, (off, size, levels) in enumerate(plans):
        c = remote(
            p_ref.at[1 - core, pl.ds(off, size)], core_in.at[pl.ds(off, size)], cs.at[k], cr.at[k], sibling
        )
        c.start()
        first.append(c)
    open_copies = []
    loss_steps = [("c", [sibling])] + [
        (a, [device_at(a, (at[a] + d) % SIZE[a]) for d in range(1, SIZE[a])]) for a in "xyz"
    ]
    loss_value = loss_ref[...]

    def loss_send(level, value):
        base = (0, 2, 6, 10)[level]
        sbase = (0, 1, 4, 7)[level]
        loss_in[base] = value
        started = []
        for d, dev in enumerate(loss_steps[level][1]):
            c = remote(loss_in.at[base], loss_in.at[base + 1 + d], ls.at[sbase + d], lr.at[sbase + d], dev)
            c.start()
            started.append(c)
        return started

    def loss_take(level, started):
        base = (0, 2, 6, 10)[level]
        for c in started:
            c.wait()
        total = loss_in[base]
        for d in range(len(started)):
            total = total + loss_in[base + 1 + d]
        return total

    loss_open = loss_send(0, loss_value)

    running = [None] * len(plans)
    for level in range(3):
        for k, (off, size, levels) in enumerate(plans):
            a, n, u = levels[level]
            send, recv, total, gather = parts[k][level]
            me = at[a]
            if level == 0:
                first[k].wait()
                send[...] = (p_ref[core, off : off + size] + core_in[off : off + size]).astype(jnp.bfloat16)
            else:
                ua = levels[level - 1][1:]
                prev_n, prev_u = ua
                pa = levels[level - 1][0]
                psend, precv, ptotal, _ = parts[k][level - 1]
                for c in running[k]:
                    c.wait_recv()
                base = at[pa] * prev_u
                if level == 1:
                    value = p_ref[core, pl.ds(off + base, prev_u)] + core_in[pl.ds(off + base, prev_u)]
                else:
                    value = ptotal[pl.ds(base, prev_u)]
                for d in range(prev_n - 1):
                    value = value + precv[d].astype(jnp.float32)
                total[0:prev_u] = value
                if n * u > prev_u:
                    total[prev_u:] = jnp.zeros((n * u - prev_u, 16, 128), jnp.float32)
                send[...] = total[...].astype(jnp.bfloat16)
            started = []
            for d in range(1, n):
                p = (me + d) % n
                c = remote(
                    send.at[pl.ds(p * u, u)],
                    recv.at[d - 1],
                    rs_s.at[k, level, d - 1],
                    rs_r.at[k, level, d - 1],
                    device_at(a, p),
                )
                c.start()
                started.append(c)
            running[k] = started
            open_copies += started
        loss_value = loss_take(level, loss_open)
        loss_open = loss_send(level + 1, loss_value)

    for level in (2, 1, 0):
        for k, (off, size, levels) in enumerate(plans):
            a, n, u = levels[level]
            send, recv, total, gather = parts[k][level]
            me = at[a]
            target = g_ref.at[core] if level == 0 else gather
            shift = off if level == 0 else 0
            mine = pl.ds(shift + me * u, u)
            if level == 2:
                for c in running[k]:
                    c.wait_recv()
                value = total[pl.ds(me * u, u)]
                for d in range(n - 1):
                    value = value + recv[d].astype(jnp.float32)
                target[mine] = value.astype(jnp.bfloat16)
                source = target.at[mine]
            else:
                below = parts[k][level + 1][3]
                for c in running[k]:
                    c.wait_recv()
                target[mine] = below[0:u]
                source = below.at[pl.ds(0, u)]
            started = []
            for d in range(1, n):
                c = remote(
                    source,
                    target.at[mine],
                    ag_s.at[k, level, d - 1],
                    ag_r.at[k, level, d - 1],
                    device_at(a, (me + d) % n),
                )
                c.start()
                started.append(c)
            running[k] = started
            open_copies += started
            if level == 0:
                c = remote(
                    g_ref.at[core, mine], g_ref.at[core, mine], cs2.at[k, 0], cr2.at[k, 0], sibling
                )
                c.start()
                open_copies.append(c)
                running[k] = (started, [c])
    loss_out[...] = loss_take(3, loss_open)
    last = []
    for d in range(1, 4):
        for k, (off, size, levels) in enumerate(plans):
            a, n, u = levels[0]
            for dd in range(d, d + 1) if d < 3 else range(3, n):
                if dd >= n:
                    continue
                started, sent = running[k]
                started[dd - 1].wait_recv()
                src = (at[a] + n - dd) % n
                piece = pl.ds(off + src * u, u)
                c = remote(g_ref.at[core, piece], g_ref.at[core, piece], cs2.at[k, dd], cr2.at[k, dd], sibling)
                c.start()
                sent.append(c)
                open_copies.append(c)
    for k in range(len(plans)):
        for c in running[k][1]:
            c.wait_recv()
    for c in open_copies:
        c.wait_send()


def total_of(partial, loss):
    plans = steps_of()
    scratch = [pltpu.VMEM((UNITS, 16, 128), jnp.float32)]
    for off, size, levels in plans:
        for a, n, u in levels:
            scratch += [
                pltpu.VMEM((n * u, 16, 128), jnp.bfloat16),
                pltpu.VMEM((n - 1, u, 16, 128), jnp.bfloat16),
                pltpu.VMEM((n * u, 16, 128), jnp.float32),
                pltpu.VMEM((n * u, 16, 128), jnp.bfloat16),
            ]
    scratch += [
        pltpu.VMEM((18, 8, 128), jnp.float32),
        pltpu.SemaphoreType.DMA((3,)),
        pltpu.SemaphoreType.DMA((3,)),
        pltpu.SemaphoreType.DMA((3, 8)),
        pltpu.SemaphoreType.DMA((3, 8)),
        pltpu.SemaphoreType.DMA((3, 3, 7)),
        pltpu.SemaphoreType.DMA((3, 3, 7)),
        pltpu.SemaphoreType.DMA((3, 3, 7)),
        pltpu.SemaphoreType.DMA((3, 3, 7)),
        pltpu.SemaphoreType.DMA((14,)),
        pltpu.SemaphoreType.DMA((14,)),
    ]
    vmem = pl.BlockSpec(memory_space=pltpu.VMEM)
    return pl.pallas_call(
        total_kernel,
        out_shape=(
            jax.ShapeDtypeStruct((2, UNITS, 16, 128), jnp.bfloat16),
            jax.ShapeDtypeStruct((8, 128), jnp.float32),
        ),
        in_specs=[vmem, vmem],
        out_specs=(vmem, vmem),
        scratch_shapes=scratch,
        compiler_params=pltpu.CompilerParams(
            collective_id=0, has_side_effects=True, vmem_limit_bytes=48 * 1024 * 1024
        ),
    )(partial, loss)


def unpack_kernel(g_ref, up_ref, down_ref, head_ref, kern_ref, gain_ref, small):
    for m, out in enumerate((up_ref, down_ref)):
        for j in range(MAIN_COLS):
            piece = g_ref[m, j * MAIN_ROWS : (j + 1) * MAIN_ROWS].astype(jnp.float32)
            out[0:640, j * 128 : (j + 1) * 128] = piece.reshape(640, 128)
        for j in range(SMALL_COLS):
            piece = g_ref[m, MAIN + j * SMALL_ROWS : MAIN + (j + 1) * SMALL_ROWS].astype(jnp.float32)
            small[m, :, j * 128 : (j + 1) * 128] = piece.reshape(64, 128)
    head_ref[0:64, :] = small[0, :, 0:641]
    head_ref[64:72, :] = small[1, 0:8, 0:641]
    kern_ref[...] = small[1, 8:33, 0:641]
    gain_ref[...] = small[1, 33:34, 0:641]
    for m, out in enumerate((up_ref, down_ref)):
        r = 34 + 5 * m
        edge = small[1, 32:56, :]
        cols = jnp.transpose(edge)[0:641, r - 32 : r - 30]
        out[:, 1280:1282] = cols
        out[640:641, 0:640] = small[1, r + 2 : r + 3, 0:640]
        out[640:641, 640:1280] = small[1, r + 3 : r + 4, 0:640]


def unpacked(g):
    vmem = pl.BlockSpec(memory_space=pltpu.VMEM)
    f32 = jnp.float32
    return pl.pallas_call(
        unpack_kernel,
        out_shape=(
            jax.ShapeDtypeStruct((641, 1282), f32),
            jax.ShapeDtypeStruct((641, 1282), f32),
            jax.ShapeDtypeStruct((72, 641), f32),
            jax.ShapeDtypeStruct((25, 641), f32),
            jax.ShapeDtypeStruct((1, 641), f32),
        ),
        in_specs=[vmem],
        out_specs=(vmem,) * 5,
        scratch_shapes=[pltpu.VMEM((2, 64, 768), f32)],
        compiler_params=pltpu.CompilerParams(vmem_limit_bytes=48 * 1024 * 1024),
    )(g)


ROWS = 2
LON = 160
CELLS = ROWS * LON
C = 641
HID = 1282
FIELDS = 72
MEMBERS = 16
NLAT = 32
BLOCK = CELLS // MEMBERS
CHUNKS = 6
DELTA = 0.1
EPSILON = 1e-05


def contract(left, right, dims):
    return lax.dot_general(left, right, ((dims[:1], dims[1:]), ((), ())), preferred_element_type=jnp.float32)


def put(ref, value):
    for c in range(CHUNKS - 1):
        ref[c] = value[:, c * 128 : (c + 1) * 128]
    ref[CHUNKS - 1, :, 0:1] = value[:, 640:641]


def member_device(m):
    return {"mem_0": m // 4, "mem_1": (m // 2) % 2, "mem_2": m % 2}


def step_kernel(
    state,
    conv_kernel,
    gain,
    up,
    down_t,
    head_t,
    target,
    field_weight,
    area,
    p_ref,
    loss_ref,
    win,
    ck,
    gn,
    su,
    nr,
    inv,
    sc,
    rd,
    pre,
    slope,
    hid,
    hp,
    fcs,
    fs,
    fr,
    truth,
    co_s,
    co_r,
    co,
    dp,
    dsum,
    dsc,
    small,
    halo_s,
    halo_r,
    fc_s,
    fc_r,
    ct_s,
    ct_r,
):
    f32, bf16 = jnp.float32, jnp.bfloat16
    lat = lax.axis_index("lat_0") * 8 + lax.axis_index("lat_1")
    member = lax.axis_index("mem_0") * 4 + lax.axis_index("mem_1") * 2 + lax.axis_index("mem_2")

    def lat_device(d):
        p = (lat + d) % 16
        return {"lat_0": p // 8, "lat_1": p % 8}

    above, below = lat_device(1), lat_device(15)
    others = [member_device((member + d) % MEMBERS) for d in range(1, MEMBERS)]
    barrier = pltpu.get_barrier_semaphore()
    for dev in [above, below] + others:
        pl.semaphore_signal(barrier, inc=1, device_id=dev, device_id_type=MESH_ID)

    def remote(src, dst, s, r, dev):
        return pltpu.make_async_remote_copy(
            src_ref=src, dst_ref=dst, send_sem=s, recv_sem=r, device_id=dev, device_id_type=MESH_ID
        )

    win[CHUNKS - 1, 2:4] = jnp.zeros((2, 176, 128), f32)
    for c in range(CHUNKS - 1):
        win[c, 2:4, 8:168, :] = state[:, :, c * 128 : (c + 1) * 128]
    win[CHUNKS - 1, 2:4, 8:168, 0:1] = state[:, :, 640:641]
    pl.semaphore_wait(barrier, 2 + len(others))

    def halo(c):
        mine = win.at[c, 2:4, 8:168]
        return (
            remote(mine, win.at[c, 0:2, 8:168], halo_s.at[0, c], halo_r.at[0, c], above),
            remote(mine, win.at[c, 4:6, 8:168], halo_s.at[1, c], halo_r.at[1, c], below),
        )

    @pl.loop(0, CHUNKS)
    def _(c):
        for copy in halo(c):
            copy.start()

    ck[CHUNKS - 1] = jnp.zeros((25, 128), f32)
    put(ck, conv_kernel[...])
    gn[CHUNKS - 1] = jnp.zeros((1, 128), f32)
    put(gn, gain[...])
    hp[:, 640:768] = jnp.zeros((FIELDS, 128), bf16)
    hp[:, 0:641] = head_t[...]
    rd[:, 640:768] = jnp.zeros((CELLS, 128), bf16)
    su[CHUNKS - 1] = jnp.zeros((CELLS, 128), f32)
    dsc[CHUNKS - 1] = jnp.zeros((CELLS, 128), f32)
    small[...] = jnp.zeros((2, CHUNKS, 64, 128), f32)
    for i in range(ROWS):
        columns = jnp.transpose(target[:, i, :])
        for b in range(MEMBERS // ROWS):
            truth[i * (MEMBERS // ROWS) + b] = columns[b * BLOCK : (b + 1) * BLOCK, :]

    def wrap(c, rows):
        win[c, rows, 6:8, :] = win[c, rows, 166:168, :]
        win[c, rows, 168:170, :] = win[c, rows, 8:10, :]

    def taps(c, i, rows, acc):
        for a in rows:
            for b in range(5):
                acc = acc + ck[c, 5 * a + b : 5 * a + b + 1, :] * win[c, i + a, 6 + b : 166 + b, :]
        return acc

    own = ((2, 3), (1, 2))
    met = ((0, 1, 4), (0, 3, 4))

    @pl.loop(0, CHUNKS)
    def _(c):
        wrap(c, slice(2, 4))
        for i in range(ROWS):
            su[c, i * LON : (i + 1) * LON] = taps(c, i, own[i], win[c, 2 + i, 8:168, :])

    @pl.loop(0, CHUNKS)
    def _(c):
        for copy in halo(c):
            copy.wait_recv()

        @pl.when(lat == 0)
        def _():
            win[c, 0:2] = jnp.zeros((2, 176, 128), f32)

        @pl.when(lat == 15)
        def _():
            win[c, 4:6] = jnp.zeros((2, 176, 128), f32)

        wrap(c, slice(0, 2))
        wrap(c, slice(4, 6))
        for i in range(ROWS):
            su[c, i * LON : (i + 1) * LON] = taps(c, i, met[i], su[c, i * LON : (i + 1) * LON])

    total = su[0]
    for c in range(1, CHUNKS):
        total = total + su[c]
    mean = jnp.sum(total, axis=1, keepdims=True) * (1.0 / C)
    first_lane = (lax.broadcasted_iota(jnp.int32, (CELLS, 128), 1) < 1).astype(f32)
    square = jnp.zeros((CELLS, 128), f32)
    for c in range(CHUNKS):
        center = su[c] - mean
        if c == CHUNKS - 1:
            center = center * first_lane
        nr[c] = center
        square = square + center * center
    inverse = lax.rsqrt(jnp.sum(square, axis=1, keepdims=True) * (1.0 / C) + EPSILON)
    inv[...] = inverse
    for c in range(CHUNKS):
        normed = nr[c] * inverse
        nr[c] = normed
        sc[:, c * 128 : (c + 1) * 128] = (normed * gn[c]).astype(bf16)

    pre[...] = jnp.dot(sc[:, 0:C], up[...], preferred_element_type=f32)

    @pl.loop(0, CELLS // 16)
    def _(r):
        rows = pl.ds(pl.multiple_of(r * 16, 16), 16)
        x = pre[rows, :]
        cumul = 0.5 * (1.0 + lax.erf(x * (1.0 / math.sqrt(2.0))))
        density = jnp.exp(-0.5 * x * x) * (1.0 / math.sqrt(2.0 * math.pi))
        hid[rows, :] = (x * cumul).astype(bf16)
        slope[rows, :] = cumul + x * density

    mlp = contract(hid[...], down_t[...], (1, 1))
    for c in range(CHUNKS - 1):
        at = slice(c * 128, (c + 1) * 128)
        rd[:, at] = (su[c] + mlp[:, at]).astype(bf16)
    rd[:, 640:641] = (su[CHUNKS - 1, :, 0:1] + mlp[:, 640:641]).astype(bf16)
    fcs[...] = contract(rd[...], hp[...], (1, 1))

    for p in range(MEMBERS):
        fs[p] = fcs[p * BLOCK : (p + 1) * BLOCK, :]
    sent = []
    for d in range(1, MEMBERS):
        p = (member + d) % MEMBERS
        c = remote(fs.at[p], fr.at[member], fc_s.at[d - 1], fc_r.at[d - 1], others[d - 1])
        c.start()
        sent.append(c)
    fr[member] = fs[member]
    for c in sent:
        c.wait_recv()

    weight = field_weight[...] * area[pl.ds(2 * lat + member // (MEMBERS // ROWS), 1), 0:FIELDS]
    against = truth[member]
    members = fr[...]
    gap = members - against[None]
    square = gap * gap + DELTA * DELTA
    root = lax.rsqrt(square)
    miss = jnp.sum(square * root - DELTA, axis=0)
    slope_miss = gap * root
    apart = jnp.zeros((BLOCK, FIELDS), f32)
    pull = jnp.zeros((MEMBERS, BLOCK, FIELDS), f32)
    for n in range(MEMBERS):
        gap = members - fr[n][None]
        square = gap * gap + DELTA * DELTA
        root = lax.rsqrt(square)
        apart = apart + jnp.sum(square * root - DELTA, axis=0)
        pull = pull + gap * root
    cells = NLAT * LON * FIELDS
    spread = miss * (1.0 / MEMBERS) - apart * (1.0 / (2.0 * MEMBERS * (MEMBERS - 1)))
    loss_ref[...] = jnp.full((8, 128), jnp.sum(weight * spread) * (1.0 / cells), f32)
    cotangent = weight[None] * (slope_miss - pull * (1.0 / (MEMBERS - 1))) * (1.0 / (MEMBERS * math.sqrt(cells)))
    co_s[...] = cotangent.astype(bf16)
    back = []
    for d in range(1, MEMBERS):
        p = (member + d) % MEMBERS
        c = remote(co_s.at[p], co_r.at[member], ct_s.at[d - 1], ct_r.at[d - 1], others[d - 1])
        c.start()
        back.append(c)
    co_r[member] = co_s[member]
    for c in back:
        c.wait_recv()
    for p in range(MEMBERS):
        fcs[p * BLOCK : (p + 1) * BLOCK, :] = co_r[p].astype(f32)
    co[...] = fcs[...].astype(bf16)

    d_output = jnp.dot(co[...], hp[...], preferred_element_type=f32)
    for c in range(CHUNKS):
        dsum[c] = d_output[:, c * 128 : (c + 1) * 128]
    d_round = d_output[:, 0:C].astype(bf16)
    pre[...] = jnp.dot(d_round, down_t[...], preferred_element_type=f32)

    @pl.loop(0, CELLS // 16)
    def _(r):
        rows = pl.ds(pl.multiple_of(r * 16, 16), 16)
        dp[rows, :] = (pre[rows, :] * slope[rows, :]).astype(bf16)

    def weight_grad(m, left, right_ref, edge_row):
        for q in range(5):
            part = contract(left, right_ref[:, q * 256 : (q + 1) * 256], (0, 0))
            for h in range(2):
                j = 2 * q + h
                lanes = slice(h * 128, (h + 1) * 128)
                p_ref[m, j * MAIN_ROWS : (j + 1) * MAIN_ROWS] = part[0:640, lanes].reshape(MAIN_ROWS, 16, 128)
                small[1, j % 5, edge_row + 2 + j // 5 : edge_row + 3 + j // 5, :] = part[640:641, lanes]
        edge = contract(right_ref[:, 1280:1282], left, (0, 0))
        for c in range(CHUNKS - 1):
            small[1, c, edge_row : edge_row + 2, :] = edge[:, c * 128 : (c + 1) * 128]
        small[1, CHUNKS - 1, edge_row : edge_row + 2, 0:1] = edge[:, 640:641]

    weight_grad(1, d_round, hid, 39)
    weight_grad(0, sc[:, 0:C], dp, 34)
    head_grad = contract(co[...], rd[...], (0, 0))
    for c in range(CHUNKS):
        small[0, c, 0:64, :] = head_grad[0:64, c * 128 : (c + 1) * 128]
        small[1, c, 0:8, :] = head_grad[64:72, c * 128 : (c + 1) * 128]
    put(dsc, contract(dp[...], up[...], (1, 1)))
    mean_a = jnp.zeros((CELLS, 128), f32)
    mean_b = jnp.zeros((CELLS, 128), f32)
    for c in range(CHUNKS):
        both = dsc[c] * nr[c]
        small[1, c, 33:34, :] = jnp.sum(both, axis=0, keepdims=True)
        mean_a = mean_a + dsc[c] * gn[c]
        mean_b = mean_b + both * gn[c]
    mean_a = jnp.sum(mean_a, axis=1, keepdims=True) * (1.0 / C)
    mean_b = jnp.sum(mean_b, axis=1, keepdims=True) * (1.0 / C)
    for c in range(CHUNKS):
        dsum[c] = dsum[c] + inv[...] * (dsc[c] * gn[c] - mean_a - nr[c] * mean_b)

    @pl.loop(0, CHUNKS)
    def _(c):
        for a in range(5):
            acc = [jnp.zeros((8, 128), f32) for _ in range(5)]
            for i in range(ROWS):
                for t in range(LON // 8):
                    d = dsum[c, i * LON + 8 * t : i * LON + 8 * t + 8, :]
                    for b in range(5):
                        acc[b] = acc[b] + d * win[c, i + a, 6 + b + 8 * t : 14 + b + 8 * t, :]
            for b in range(5):
                tap = 8 + 5 * a + b
                small[1, c, tap : tap + 1, :] = jnp.sum(acc[b], axis=0, keepdims=True)

    for m in range(2):
        for c in range(CHUNKS):
            p_ref[m, MAIN + c * SMALL_ROWS : MAIN + (c + 1) * SMALL_ROWS] = small[m, c].reshape(SMALL_ROWS, 16, 128)

    @pl.loop(0, CHUNKS)
    def _(c):
        for copy in halo(c):
            copy.wait_send()

    for c in sent + back:
        c.wait_send()


def gradients(state, conv_kernel, gain, up, down_t, head_t, target, field_weight, area):
    f32, bf16 = jnp.float32, jnp.bfloat16
    vmem = pl.BlockSpec(memory_space=pltpu.VMEM)
    V = pltpu.VMEM
    dma = pltpu.SemaphoreType.DMA
    return pl.pallas_call(
        step_kernel,
        out_shape=(
            jax.ShapeDtypeStruct((2, UNITS, 16, 128), f32),
            jax.ShapeDtypeStruct((8, 128), f32),
        ),
        in_specs=[vmem] * 9,
        out_specs=(vmem, vmem),
        scratch_shapes=[
            V((CHUNKS, 6, 176, 128), f32),
            V((CHUNKS, 25, 128), f32),
            V((CHUNKS, 1, 128), f32),
            V((CHUNKS, CELLS, 128), f32),
            V((CHUNKS, CELLS, 128), f32),
            V((CELLS, 1), f32),
            V((CELLS, 768), bf16),
            V((CELLS, 768), bf16),
            V((CELLS, HID), f32),
            V((CELLS, HID), f32),
            V((CELLS, HID), bf16),
            V((FIELDS, 768), bf16),
            V((CELLS, FIELDS), f32),
            V((MEMBERS, BLOCK, FIELDS), f32),
            V((MEMBERS, BLOCK, FIELDS), f32),
            V((MEMBERS, BLOCK, FIELDS), f32),
            V((MEMBERS, BLOCK, FIELDS), bf16),
            V((MEMBERS, BLOCK, FIELDS), bf16),
            V((CELLS, FIELDS), bf16),
            V((CELLS, HID), bf16),
            V((CHUNKS, CELLS, 128), f32),
            V((CHUNKS, CELLS, 128), f32),
            V((2, CHUNKS, 64, 128), f32),
            dma((2, CHUNKS)),
            dma((2, CHUNKS)),
            dma((MEMBERS - 1,)),
            dma((MEMBERS - 1,)),
            dma((MEMBERS - 1,)),
            dma((MEMBERS - 1,)),
        ],
        compiler_params=pltpu.CompilerParams(
            collective_id=1, has_side_effects=True, vmem_limit_bytes=56 * 1024 * 1024
        ),
    )(state, conv_kernel, gain, up, down_t, head_t, target, field_weight, area)


def local(
    state, conv_kernel, norm_gain, up_weight, down_weight, field_head_weight, target, field_weight
):
    rows = (np.arange(NLAT, dtype=np.float32) + np.float32(0.5)) / np.float32(NLAT) - np.float32(1.0)
    area = np.broadcast_to(np.cos(np.float32(0.5 * math.pi) * rows)[:, None], (NLAT, 128))
    partial, loss = gradients(
        jnp.transpose(state[0], (1, 2, 0)),
        conv_kernel,
        norm_gain[None],
        up_weight,
        down_weight.T,
        field_head_weight.T,
        target,
        field_weight[None],
        jnp.asarray(area, jnp.float32),
    )
    total, loss_total = total_of(partial, loss)
    up, down_t, head_t, kern, gain_row = unpacked(total)
    return (loss_total[0, 0], kern, gain_row[0], up, down_t.T, head_t.T)


def solution(mesh):
    finer = Mesh(mesh.devices.reshape(4, 2, 2, 2, 8), AXES)
    mem, lat = AXES[:3], AXES[3:]
    in_specs = (P(mem, None, lat, None), P(), P(), P(), P(), P(), P(None, lat, None), P())
    out_specs = (P(), P(), P(), P(), P(), P())
    return jax.shard_map(local, mesh=finer, in_specs=in_specs, out_specs=out_specs, check_vma=False)
```

time: 207 us -> 124 us (0.60)
  Pallas kernels: 70.3 us -> 119 us
  local copies, waits for them, and re-layouts: 44.6 us -> 3.79 us
  other arithmetic: 27.7 us -> 0.6 us
  waiting for transfers between devices: 20.1 us -> 0 us
  starting transfers between devices: 16 us -> 0 us
  matrix products: 12.9 us -> 0 us
  blocking collectives: 12 us -> 0 us
    pallas_call x0 -> x1, Pallas kernels: none -> 62.4 us  [gradients(): pl.pallas_call(step_kernel, out_shape=(jax.ShapeDtypeStruct((2, UNITS, 16...]
    reduce_sum x8 -> x0, other arithmetic: 14.1 us -> none  [the longest x1 5.94 us: forward_apply(): center = summed - jnp.mean(summed, axis=0)]
    pallas_call x1, Pallas kernels: 66.8 us -> 53 us  [total_of(): pl.pallas_call(total_kernel, out_shape=(jax.ShapeDtypeStruct((2, UNITS, 1...]
    dot_general x9 -> x0, matrix products: 12.9 us -> none  [the longest x3 3.62 us: tail_dot(): lax.dot_general(left, right, (((1,), (1,)), ((), ())), preferred_element_...]
    all_to_all x2 -> x0, blocking collectives: 12 us -> none  [moved_by_axis(): lax.all_to_all(pieces, axes[k], split_axis=k, concat_axis=k, tiled=True)]
    ppermute x2 -> x0, waiting for transfers between devices: 11.6 us -> none  [the longest x1 10.6 us: extended(): lax.ppermute(head, axis, [((i + 1) % count, i) for i in range(ends)])]
    slice x14 -> x0, local copies, waits for them, and re-layouts: 11.5 us -> none  [the longest x2 5.14 us: stencil(): shifted = jnp.roll(window, 2 - col_off, axis=2)]
    reshape x5 -> x0, local copies, waits for them, and re-layouts: 9.94 us -> none  [the longest x2 9.82 us: main(): g[:640, :1280].reshape(40, 16, 10, 128).transpose(0, 2, 1, 3)]
  transfers between devices with their start and end apart: 4 -> 0, of which waited for: 4 -> 0; matrix products, arithmetic and copies ran while one was open for 4% -> 0% of each run, Pallas kernels for 0% -> 0%
where the time goes in v2:
time: 124 us
  Pallas kernels  119 us (96%)
  local copies, waits for them, and re-layouts  3.79 us (3%)
    pallas_call x1, Pallas kernels, gradients(): pl.pallas_call(step_kernel, out_shape=(jax.ShapeDtypeStruct((2, UNITS, 16...  62.4 us
    pallas_call x1, Pallas kernels, total_of(): pl.pallas_call(total_kernel, out_shape=(jax.ShapeDtypeStruct((2, UNITS, 1...  53 us
    pallas_call x1, Pallas kernels, unpacked(): pl.pallas_call(unpack_kernel, out_shape=(jax.ShapeDtypeStruct((641, 1282)...  3.54 us

profile of v2, /device:TPU:1, one launch (start us, length us, event | category | flops | bytes accessed | tf_op | source)
XLA Modules:
  0.0 123.9 jit_solution(15189895312827405140)
XLA Ops:
  0.6 1.3 %broadcast_in_dim.6.gain = f32[1,641]{1,0:T(1,128)} reshape(f32[641]{0:T(1024)} %param.11) | data formatting | bytes 5128 | tf_op jit(solution)/shard_map/broadcast_in_dim | solution.py:677
  1.9 1.3 %jit_solution_.3.area = f32[32,128]{1,0:T(8,128)} broadcast(f32[32]{0:T(128)} %constant.2.clone), dimensions={0} | broadcast | bytes 16512 | tf_op jit(solution)
  3.2 62.4 %shard_map.136 = (f32[2,424,16,128]{3,2,1,0:T(8,128)}, f32[8,128]{1,0:T(8,128)}) custom-call(f32[2,160,641]{2,1,0:T(8,128)} %bitcast.10, f32[25,641]{1,0:T(8,128)} %conv_kernel.1, f32[1,641]{1,0:T(1,128)} %broadcast_in_dim.6.gain, bf16[641,1282]{1,0:T(8,128)(2,1)} %up.1, bf16[641,1282]{1,0:T(8,128)(2,1)} %bitcast.9, bf16[72,641]{1,0:T(8,128)(2,1)} %bitcast.11, ...), custom_call_target="tpu_custom_call" | custom-call | tf_op jit(solution)/shard_map/pallas_call | solution.py:624
  65.6 0.0 copy-start
  65.6 0.7 copy-done
  66.3 53.0 %shard_map.137 = (bf16[2,424,16,128]{3,2,1,0:T(8,128)(2,1)S(1)}, f32[8,128]{1,0:T(8,128)S(1)}) custom-call(f32[2,424,16,128]{3,2,1,0:T(8,128)} %get-tuple-element.15.p_ref, f32[8,128]{1,0:T(8,128)S(1)} %copy-done), custom_call_target="tpu_custom_call" | custom-call | tf_op jit(solution)/shard_map/pallas_call | solution.py:253
  119.3 0.5 slice.3
  119.8 3.5 %shard_map.138 = (f32[641,1282]{1,0:T(8,128)}, f32[641,1282]{1,0:T(8,128)}, f32[72,641]{1,0:T(8,128)}, f32[25,641]{1,0:T(8,128)}, f32[1,641]{1,0:T(1,128)S(1)}) custom-call(bf16[2,424,16,128]{3,2,1,0:T(8,128)(2,1)S(1)} %get-tuple-element.18.g_ref), custom_call_target="tpu_custom_call" | custom-call | tf_op jit(solution)/shard_map/pallas_call | solution.py:292
  123.3 0.6 reduce
Async XLA Ops:
  65.6 0.7 copy-start

commit v3 on v2

v3 whole, which is shorter than its diff:
```python
import math

import jax
import jax.numpy as jnp
import numpy as np
from jax import lax
from jax.experimental import pallas as pl
from jax.experimental.pallas import tpu as pltpu
from jax.sharding import Mesh
from jax.sharding import PartitionSpec as P

AXES = ("mem_0", "mem_1", "mem_2", "lat_0", "lat_1")
MESH_ID = pl.DeviceIdType.MESH
ROWS = 2
LON = 160
CELLS = ROWS * LON
C = 641
HID = 1282
FIELDS = 72
MEMBERS = 16
NLAT = 32
BLOCK = CELLS // MEMBERS
CHUNKS = 6
DELTA = 0.1
EPSILON = 1e-05
AREA = np.cos(
    np.float32(0.5 * math.pi)
    * ((np.arange(NLAT, dtype=np.float32) + np.float32(0.5)) / np.float32(NLAT) - np.float32(1.0))
)

TALL, WIDE = 40, 5
HALF = TALL * WIDE
SMALL = 2 * HALF
SMALL_TALL = 4
UNITS = SMALL + SMALL_TALL * CHUNKS
SIZE = {"x": 4, "y": 4, "z": 8}
PARTS = ((0, 192, "xyz", True), (192, 192, "yxz", True), (384, 40, "xyz", False))


def steps_of(size, order):
    levels = []
    for a in order:
        size = -(-size // SIZE[a])
        levels.append((a, SIZE[a], size))
    return levels


PLANS = tuple((off, size, steps_of(size, order), relay) for off, size, order, relay in PARTS)


def contract(left, right, dims):
    return lax.dot_general(left, right, ((dims[:1], dims[1:]), ((), ())), preferred_element_type=jnp.float32)


def put(ref, value):
    for c in range(CHUNKS - 1):
        ref[c] = value[:, c * 128 : (c + 1) * 128]
    ref[CHUNKS - 1, :, 0:1] = value[:, 640:641]


def member_device(m):
    return {"mem_0": m // 4, "mem_1": (m // 2) % 2, "mem_2": m % 2}


def device_at(axis, p):
    if axis == "x":
        return {"mem_0": p}
    if axis == "y":
        return {"lat_0": p // 2, "mem_1": p % 2}
    return {"lat_1": p}


def remote(src, dst, s, r, dev):
    return pltpu.make_async_remote_copy(
        src_ref=src, dst_ref=dst, send_sem=s, recv_sem=r, device_id=dev, device_id_type=MESH_ID
    )


class Total:
    def __init__(self, g_ref, own, away, core_in, parts, loss_in, sems):
        self.g, self.own, self.away, self.core_in, self.parts, self.loss_in = g_ref, own, away, core_in, parts, loss_in
        self.sems = sems
        self.core = lax.axis_index("mem_2")
        self.sibling = {"mem_2": 1 - self.core}
        self.at = {
            "x": lax.axis_index("mem_0"),
            "y": lax.axis_index("lat_0") * 2 + lax.axis_index("mem_1"),
            "z": lax.axis_index("lat_1"),
        }
        self.open = []
        self.first = {}
        self.running = {}

    def peers(self):
        out = []
        for a in "yz":
            out += [device_at(a, (self.at[a] + d) % SIZE[a]) for d in range(1, SIZE[a])]
        return out

    def begin(self, src, dst, s, r, dev):
        c = remote(src, dst, s, r, dev)
        c.start()
        self.open.append(c)
        return c

    def loss_send(self, level, value):
        base, sbase = (0, 2, 6, 10)[level], (0, 1, 4, 7)[level]
        ls, lr = self.sems["loss"]
        if level == 0:
            devices = [self.sibling]
        else:
            a = "xyz"[level - 1]
            devices = [device_at(a, (self.at[a] + d) % SIZE[a]) for d in range(1, SIZE[a])]
        self.loss_in[base] = value
        self.loss_open = [
            self.begin(self.loss_in.at[base], self.loss_in.at[base + 1 + d], ls.at[sbase + d], lr.at[sbase + d], dev)
            for d, dev in enumerate(devices)
        ]

    def loss_take(self, level):
        base = (0, 2, 6, 10)[level]
        for c in self.loss_open:
            c.wait_recv()
        total = self.loss_in[base]
        for d in range(len(self.loss_open)):
            total = total + self.loss_in[base + 1 + d]
        return total

    def loss_next(self, level):
        self.loss_send(level + 1, self.loss_take(level))

    def pair(self, k):
        off, size = PLANS[k][:2]
        s, r = self.sems["pair"]
        units = pl.ds(off, size)
        self.first[k] = self.begin(self.away.at[units], self.core_in.at[units], s.at[k], r.at[k], self.sibling)

    def held(self, start, count):
        return self.own[pl.ds(start, count)] + self.core_in[pl.ds(start, count)]

    def scatter_first(self, k):
        off, size, levels, relay = PLANS[k]
        a, n, u = levels[0]
        send, recv = self.parts[k][0][:2]
        self.first[k].wait_recv()
        send[...] = self.held(off, size).astype(jnp.bfloat16)
        if not relay:
            self.scatter_sends(k, 0)
            return
        s, r = self.sems["relay"]
        h = u // 2
        me = self.at[a]
        up, down, far = (me + 1) % n, (me + n - 1) % n, (me + 2) % n
        into = self.parts[k][0][4]
        dev_up, dev_down = device_at(a, up), device_at(a, down)
        b = lambda i, src, dst, dev: self.begin(src, dst, s.at[k, i], r.at[k, i], dev)
        self.running[k] = [
            b(0, send.at[pl.ds(far * u, h)], into.at[0], dev_up),
            b(1, send.at[pl.ds(far * u + h, h)], into.at[1], dev_down),
            b(2, send.at[pl.ds(up * u + h, h)], recv.at[0, pl.ds(h, h)], dev_up),
            b(3, send.at[pl.ds(down * u, h)], recv.at[1, pl.ds(0, h)], dev_down),
        ]

    def relay(self, k):
        off, size, levels, _ = PLANS[k]
        a, n, u = levels[0]
        recv, into, outof = self.parts[k][0][1], self.parts[k][0][4], self.parts[k][0][5]
        s, r = self.sems["relay"]
        h = u // 2
        me = self.at[a]
        up, down = (me + 1) % n, (me + n - 1) % n
        for i, (dev, start, half) in enumerate(((up, off + up * u, 0), (down, off + down * u + h, h))):
            self.running[k][i].wait_recv()
            outof[i] = (self.held(start, h) + into[i].astype(jnp.float32)).astype(jnp.bfloat16)
            self.running[k].append(
                self.begin(outof.at[i], recv.at[i, pl.ds(half, h)], s.at[k, 4 + i], r.at[k, 4 + i], device_at(a, dev))
            )
        self.running[k] = self.running[k][2:]

    def scatter_sends(self, k, level):
        a, n, u = PLANS[k][2][level]
        send, recv = self.parts[k][level][:2]
        s, r = self.sems["scatter"]
        self.running[k] = []
        for d in range(1, n):
            p = (self.at[a] + d) % n
            self.running[k].append(
                self.begin(
                    send.at[pl.ds(p * u, u)], recv.at[d - 1], s.at[k, level, d - 1], r.at[k, level, d - 1], device_at(a, p)
                )
            )

    def gathered_sum(self, k, level):
        off, size, levels, relay = PLANS[k]
        a, n, u = levels[level]
        recv, total = self.parts[k][level][1:3]
        for c in self.running[k]:
            c.wait_recv()
        me = self.at[a]
        value = self.held(off + me * u, u) if level == 0 else total[pl.ds(me * u, u)]
        for d in range(2 if relay and level == 0 else n - 1):
            value = value + recv[d].astype(jnp.float32)
        return value

    def scatter(self, k, level):
        a, n, u = PLANS[k][2][level]
        below = PLANS[k][2][level - 1][2]
        send, recv, total = self.parts[k][level][:3]
        total[0:below] = self.gathered_sum(k, level - 1)
        if n * u > below:
            total[below:] = jnp.zeros((n * u - below, 16, 128), jnp.float32)
        send[...] = total[...].astype(jnp.bfloat16)
        self.scatter_sends(k, level)

    def gather(self, k, level):
        a, n, u = PLANS[k][2][level]
        into = self.parts[k][level][3]
        me = self.at[a]
        mine = pl.ds(me * u, u)
        s, r = self.sems["gather"]
        if level == 2:
            into[mine] = self.gathered_sum(k, 2).astype(jnp.bfloat16)
            source = into.at[mine]
        else:
            below = self.parts[k][level + 1][3]
            for c in self.running[k]:
                c.wait_recv()
            into[mine] = below[0:u]
            source = below.at[pl.ds(0, u)]
        self.running[k] = [
            self.begin(
                source, into.at[mine], s.at[k, level, d - 1], r.at[k, level, d - 1], device_at(a, (me + d) % n)
            )
            for d in range(1, n)
        ]

    def to_sibling(self, k, i, start, count):
        s, r = self.sems["back"]
        piece = self.g.at[self.core, pl.ds(start, count)]
        self.last.append(self.begin(piece, piece, s.at[k, i], r.at[k, i], self.sibling))

    last = None

    def gather_last(self):
        self.last = []
        s, r = self.sems["gather"]
        s2, r2 = self.sems["relay_back"]
        flights = {}
        for k, (off, size, levels, relay) in enumerate(PLANS):
            a, n, u = levels[0]
            me = self.at[a]
            below = self.parts[k][1][3]
            for c in self.running[k]:
                c.wait_recv()
            mine = pl.ds(off + me * u, u)
            self.g[self.core, mine] = below[0:u]
            if relay:
                h = u // 2
                up, down = device_at(a, (me + 1) % n), device_at(a, (me + n - 1) % n)
                lo, hi = pl.ds(off + me * u, h), pl.ds(off + me * u + h, h)
                b = lambda i, part, src, dev: self.begin(
                    src, self.g.at[self.core, part], s2.at[k, i], r2.at[k, i], dev
                )
                flights[k] = [
                    b(0, lo, below.at[pl.ds(0, h)], up),
                    b(1, hi, below.at[pl.ds(h, h)], down),
                    b(2, hi, below.at[pl.ds(h, h)], up),
                    b(3, lo, below.at[pl.ds(0, h)], down),
                ]
            else:
                flights[k] = [
                    self.begin(
                        below.at[pl.ds(0, u)],
                        self.g.at[self.core, mine],
                        s.at[k, 0, d - 1],
                        r.at[k, 0, d - 1],
                        device_at(a, (me + d) % n),
                    )
                    for d in range(1, n)
                ]
            self.to_sibling(k, 0, off + me * u, u)
        for k, (off, size, levels, relay) in enumerate(PLANS):
            a, n, u = levels[0]
            me = self.at[a]
            if not relay:
                continue
            h = u // 2
            up, down = (me + 1) % n, (me + n - 1) % n
            for i, (start, dev) in enumerate(((off + down * u, up), (off + up * u + h, down))):
                flights[k][i].wait_recv()
                piece = self.g.at[self.core, pl.ds(start, h)]
                flights[k].append(
                    self.begin(piece, piece, s2.at[k, 4 + i], r2.at[k, 4 + i], device_at(a, dev))
                )
                self.to_sibling(k, 1 + i, start, h)
        for k, (off, size, levels, relay) in enumerate(PLANS):
            a, n, u = levels[0]
            me = self.at[a]
            h = u // 2
            up, down, far = (me + 1) % n, (me + n - 1) % n, (me + 2) % n
            if relay:
                starts = (off + down * u + h, off + up * u, off + far * u, off + far * u + h)
                for i, start in enumerate(starts):
                    flights[k][2 + i].wait_recv()
                    self.to_sibling(k, 3 + i, start, h)
            else:
                for d in range(1, n):
                    flights[k][d - 1].wait_recv()
                    self.to_sibling(k, d, off + ((me + n - d) % n) * u, u)
        for c in self.last:
            c.wait_recv()


def total_scratch():
    bf16, f32 = jnp.bfloat16, jnp.float32
    V = pltpu.VMEM
    parts = []
    for off, size, levels, relay in PLANS:
        part = []
        for level, (a, n, u) in enumerate(levels):
            relays = relay and level == 0
            one = [
                V((n * u, 16, 128), bf16),
                V((2 if relays else n - 1, u, 16, 128), bf16),
                V((n * u if level else 1, 16, 128), f32),
                V((n * u if level else 1, 16, 128), bf16),
            ]
            if relays:
                one += [V((2, u // 2, 16, 128), bf16), V((2, u // 2, 16, 128), bf16)]
            part.append(one)
        parts.append(part)
    dma = pltpu.SemaphoreType.DMA
    sems = {
        "pair": (dma((3,)), dma((3,))),
        "relay": (dma((3, 6)), dma((3, 6))),
        "relay_back": (dma((3, 6)), dma((3, 6))),
        "scatter": (dma((3, 3, 7)), dma((3, 3, 7))),
        "gather": (dma((3, 3, 7)), dma((3, 3, 7))),
        "back": (dma((3, 7)), dma((3, 7))),
        "loss": (dma((14,)), dma((14,))),
    }
    return dict(
        own=V((UNITS, 16, 128), f32),
        away=V((UNITS, 16, 128), f32),
        core_in=V((UNITS, 16, 128), f32),
        parts=parts,
        loss_in=V((18, 8, 128), f32),
        sems=sems,
    )


def step_kernel(
    state,
    conv_kernel,
    gain,
    up_hbm,
    down_hbm,
    head_t,
    target,
    field_weight,
    g_ref,
    loss_ref,
    w,
    total_refs,
):
    win, ck, gn, su, nr, inv, sc, rd = (w[i] for i in ("win", "ck", "gn", "su", "nr", "inv", "sc", "rd"))
    pre, slope, hid, hp, fcs, fs, fr = (w[i] for i in ("pre", "slope", "hid", "hp", "fcs", "fs", "fr"))
    truth, co_s, co_r, co, dp, dsum, dsc = (w[i] for i in ("truth", "co_s", "co_r", "co", "dp", "dsum", "dsc"))
    small, thin_s, thin_r, up, down_t, drr = (w[i] for i in ("small", "thin_s", "thin_r", "up", "down_t", "drr"))
    halo_s, halo_r, fc_s, fc_r, ct_s, ct_r, wt = (w[i] for i in ("halo_s", "halo_r", "fc_s", "fc_r", "ct_s", "ct_r", "wt"))
    total = Total(g_ref, **total_refs)
    f32, bf16 = jnp.float32, jnp.bfloat16
    lat = lax.axis_index("lat_0") * 8 + lax.axis_index("lat_1")
    member = lax.axis_index("mem_0") * 4 + lax.axis_index("mem_1") * 2 + lax.axis_index("mem_2")

    def lat_device(d):
        p = (lat + d) % 16
        return {"lat_0": p // 8, "lat_1": p % 8}

    above, below = lat_device(1), lat_device(15)
    others = [member_device((member + d) % MEMBERS) for d in range(1, MEMBERS)]
    barrier = pltpu.get_barrier_semaphore()
    greeted = [above, below] + others + total.peers()
    for dev in greeted:
        pl.semaphore_signal(barrier, inc=1, device_id=dev, device_id_type=MESH_ID)
    weights = [pltpu.make_async_copy(up_hbm, up, wt.at[0]), pltpu.make_async_copy(down_hbm, down_t, wt.at[1])]
    for c in weights:
        c.start()

    win[CHUNKS - 1] = jnp.zeros((6, 176, 128), f32)
    for c in range(CHUNKS - 1):
        win[c, 2:4, 8:168, :] = state[:, :, c * 128 : (c + 1) * 128]
    win[CHUNKS - 1, 2:4, 8:168, 0:1] = state[:, :, 640:641]
    thin_s[...] = jnp.zeros((8, LON), f32)
    for i in range(ROWS):
        thin_s[i : i + 1, :] = jnp.transpose(win[CHUNKS - 1, 2 + i, 8:168, :])[0:1, :]
    pl.semaphore_wait(barrier, len(greeted))

    def halo(c):
        mine = win.at[c, 2:4, 8:168]
        return (
            remote(mine, win.at[c, 0:2, 8:168], halo_s.at[0, c], halo_r.at[0, c], above),
            remote(mine, win.at[c, 4:6, 8:168], halo_s.at[1, c], halo_r.at[1, c], below),
        )

    thin = (
        remote(thin_s, thin_r.at[0], halo_s.at[0, CHUNKS - 1], halo_r.at[0, CHUNKS - 1], above),
        remote(thin_s, thin_r.at[1], halo_s.at[1, CHUNKS - 1], halo_r.at[1, CHUNKS - 1], below),
    )
    for copy in thin:
        copy.start()

    @pl.loop(0, CHUNKS - 1)
    def _(c):
        for copy in halo(c):
            copy.start()

    ck[CHUNKS - 1] = jnp.zeros((25, 128), f32)
    put(ck, conv_kernel[...])
    gn[CHUNKS - 1] = jnp.zeros((1, 128), f32)
    put(gn, gain[...].reshape(1, C))
    hp[:, 640:768] = jnp.zeros((FIELDS, 128), bf16)
    hp[:, 0:641] = head_t[...]
    rd[:, 640:768] = jnp.zeros((CELLS, 128), bf16)
    su[CHUNKS - 1] = jnp.zeros((CELLS, 128), f32)
    dsc[CHUNKS - 1] = jnp.zeros((CELLS, 128), f32)
    small[...] = jnp.zeros((2, CHUNKS, 64, 128), f32)
    for i in range(ROWS):
        columns = jnp.transpose(target[:, i, :])
        for b in range(MEMBERS // ROWS):
            truth[i * (MEMBERS // ROWS) + b] = columns[b * BLOCK : (b + 1) * BLOCK, :]

    def wrap(c, rows):
        win[c, rows, 6:8, :] = win[c, rows, 166:168, :]
        win[c, rows, 168:170, :] = win[c, rows, 8:10, :]

    def taps(c, i, rows, acc):
        for a in rows:
            for b in range(5):
                acc = acc + ck[c, 5 * a + b : 5 * a + b + 1, :] * win[c, i + a, 6 + b : 166 + b, :]
        return acc

    own = ((2, 3), (1, 2))
    met = ((0, 1, 4), (0, 3, 4))

    @pl.loop(0, CHUNKS)
    def _(c):
        wrap(c, slice(2, 4))
        for i in range(ROWS):
            su[c, i * LON : (i + 1) * LON] = taps(c, i, own[i], win[c, 2 + i, 8:168, :])

    def meet(c):
        @pl.when(lat == 0)
        def _():
            win[c, 0:2] = jnp.zeros((2, 176, 128), f32)

        @pl.when(lat == 15)
        def _():
            win[c, 4:6] = jnp.zeros((2, 176, 128), f32)

        wrap(c, slice(0, 2))
        wrap(c, slice(4, 6))
        for i in range(ROWS):
            su[c, i * LON : (i + 1) * LON] = taps(c, i, met[i], su[c, i * LON : (i + 1) * LON])

    for side, copy in enumerate(thin):
        copy.wait_recv()
        column = jnp.transpose(thin_r[side])
        for i in range(ROWS):
            win[CHUNKS - 1, 4 * side + i, 8:168, 0:1] = column[:, i : i + 1]
    meet(CHUNKS - 1)

    @pl.loop(0, CHUNKS - 1)
    def _(c):
        for copy in halo(c):
            copy.wait_recv()
        meet(c)

    level = su[0]
    for c in range(1, CHUNKS):
        level = level + su[c]
    mean = jnp.sum(level, axis=1, keepdims=True) * (1.0 / C)
    first_lane = (lax.broadcasted_iota(jnp.int32, (CELLS, 128), 1) < 1).astype(f32)
    square = jnp.zeros((CELLS, 128), f32)
    for c in range(CHUNKS):
        center = su[c] - mean
        if c == CHUNKS - 1:
            center = center * first_lane
        nr[c] = center
        square = square + center * center
    inverse = lax.rsqrt(jnp.sum(square, axis=1, keepdims=True) * (1.0 / C) + EPSILON)
    inv[...] = inverse
    for c in range(CHUNKS):
        normed = nr[c] * inverse
        nr[c] = normed
        sc[:, c * 128 : (c + 1) * 128] = (normed * gn[c]).astype(bf16)

    for c in weights:
        c.wait()
    pre[...] = jnp.dot(sc[:, 0:C], up[...], preferred_element_type=f32)

    @pl.loop(0, CELLS // 16)
    def _(r):
        rows = pl.ds(pl.multiple_of(r * 16, 16), 16)
        x = pre[rows, :]
        cumul = 0.5 * (1.0 + lax.erf(x * (1.0 / math.sqrt(2.0))))
        density = jnp.exp(-0.5 * x * x) * (1.0 / math.sqrt(2.0 * math.pi))
        hid[rows, :] = (x * cumul).astype(bf16)
        slope[rows, :] = cumul + x * density

    mlp = contract(hid[...], down_t[...], (1, 1))
    for c in range(CHUNKS - 1):
        at = slice(c * 128, (c + 1) * 128)
        rd[:, at] = (su[c] + mlp[:, at]).astype(bf16)
    rd[:, 640:641] = (su[CHUNKS - 1, :, 0:1] + mlp[:, 640:641]).astype(bf16)
    fcs[...] = contract(rd[...], hp[...], (1, 1))

    for p in range(MEMBERS):
        fs[p] = fcs[p * BLOCK : (p + 1) * BLOCK, :]
    sent = []
    for d in range(1, MEMBERS):
        p = (member + d) % MEMBERS
        c = remote(fs.at[p], fr.at[member], fc_s.at[d - 1], fc_r.at[d - 1], others[d - 1])
        c.start()
        sent.append(c)
    fr[member] = fs[member]
    for c in sent:
        c.wait_recv()

    row = 2 * lat + member // (MEMBERS // ROWS)
    area = jnp.float32(AREA[0])
    for i in range(1, NLAT):
        area = jnp.where(row == i, jnp.float32(AREA[i]), area)
    weight = field_weight[...] * area
    against = truth[member]
    members = fr[...]
    gap = members - against[None]
    square = gap * gap + DELTA * DELTA
    root = lax.rsqrt(square)
    miss = jnp.sum(square * root - DELTA, axis=0)
    slope_miss = gap * root
    apart = jnp.zeros((BLOCK, FIELDS), f32)
    pull = jnp.zeros((MEMBERS, BLOCK, FIELDS), f32)
    for n in range(MEMBERS):
        gap = members - fr[n][None]
        square = gap * gap + DELTA * DELTA
        root = lax.rsqrt(square)
        apart = apart + jnp.sum(square * root - DELTA, axis=0)
        pull = pull + gap * root
    cells = NLAT * LON * FIELDS
    spread = miss * (1.0 / MEMBERS) - apart * (1.0 / (2.0 * MEMBERS * (MEMBERS - 1)))
    cotangent = weight[None] * (slope_miss - pull * (1.0 / (MEMBERS - 1))) * (1.0 / (MEMBERS * math.sqrt(cells)))
    co_s[...] = cotangent.astype(bf16)
    back = []
    for d in range(1, MEMBERS):
        p = (member + d) % MEMBERS
        c = remote(co_s.at[p], co_r.at[member], ct_s.at[d - 1], ct_r.at[d - 1], others[d - 1])
        c.start()
        back.append(c)
    co_r[member] = co_s[member]
    total.loss_send(0, jnp.full((8, 128), jnp.sum(weight * spread) * (1.0 / cells), f32))
    for c in back:
        c.wait_recv()
    for p in range(MEMBERS):
        fcs[p * BLOCK : (p + 1) * BLOCK, :] = co_r[p].astype(f32)
    co[...] = fcs[...].astype(bf16)

    d_output = jnp.dot(co[...], hp[...], preferred_element_type=f32)
    for c in range(CHUNKS):
        dsum[c] = d_output[:, c * 128 : (c + 1) * 128]
    drr[...] = d_output.astype(bf16)

    def half_grad(base, left, right, which, out):
        for s, wide in ((0, 256), (256, 256), (512, 128)):
            columns = pl.ds(pl.multiple_of(which * 640 + s, 128), wide)
            part = contract(left[:, 0:640], right[:, columns], (0, 0))
            for h in range(wide // 128):
                j = base + (s // 128 + h) * TALL
                out[j : j + TALL] = part[:, h * 128 : (h + 1) * 128].reshape(TALL, 16, 128)

    def edge_grad(left, right, r):
        line = contract(left[:, 640:641], right[...], (0, 0))
        for j in range(2 * WIDE):
            small[1, j % 5, r + 2 + j // 5 : r + 3 + j // 5, :] = line[:, j * 128 : (j + 1) * 128]
        edge = contract(right[:, 1280:1282], left[...], (0, 0))
        for c in range(CHUNKS):
            small[1, c, r : r + 2, :] = edge[:, c * 128 : (c + 1) * 128]

    core = total.core
    half_grad(0, drr, hid, 1 - core, total.away)
    total.pair(0)
    half_grad(0, drr, hid, core, total.own)
    pre[...] = jnp.dot(drr[:, 0:C], down_t[...], preferred_element_type=f32)

    @pl.loop(0, CELLS // 16)
    def _(r):
        rows = pl.ds(pl.multiple_of(r * 16, 16), 16)
        dp[rows, :] = (pre[rows, :] * slope[rows, :]).astype(bf16)

    half_grad(HALF, sc, dp, 1 - core, total.away)
    total.pair(1)
    total.scatter_first(0)
    half_grad(HALF, sc, dp, core, total.own)
    total.loss_next(0)
    edge_grad(drr, hid, 39)
    edge_grad(sc, dp, 34)
    head_grad = contract(co[...], rd[...], (0, 0))
    for c in range(CHUNKS):
        small[0, c, 0:64, :] = head_grad[0:64, c * 128 : (c + 1) * 128]
        small[1, c, 0:8, :] = head_grad[64:72, c * 128 : (c + 1) * 128]
    total.scatter_first(1)
    put(dsc, contract(dp[...], up[...], (1, 1)))
    mean_a = jnp.zeros((CELLS, 128), f32)
    mean_b = jnp.zeros((CELLS, 128), f32)
    for c in range(CHUNKS):
        both = dsc[c] * nr[c]
        small[1, c, 33:34, :] = jnp.sum(both, axis=0, keepdims=True)
        mean_a = mean_a + dsc[c] * gn[c]
        mean_b = mean_b + both * gn[c]
    mean_a = jnp.sum(mean_a, axis=1, keepdims=True) * (1.0 / C)
    mean_b = jnp.sum(mean_b, axis=1, keepdims=True) * (1.0 / C)
    for c in range(CHUNKS):
        dsum[c] = dsum[c] + inv[...] * (dsc[c] * gn[c] - mean_a - nr[c] * mean_b)

    total.relay(0)
    total.loss_next(1)

    @pl.loop(0, CHUNKS)
    def _(c):
        for a in range(5):
            acc = [jnp.zeros((8, 128), f32) for _ in range(5)]
            for i in range(ROWS):
                for t in range(LON // 8):
                    d = dsum[c, i * LON + 8 * t : i * LON + 8 * t + 8, :]
                    for b in range(5):
                        acc[b] = acc[b] + d * win[c, i + a, 6 + b + 8 * t : 14 + b + 8 * t, :]
            for b in range(5):
                tap = 8 + 5 * a + b
                small[1, c, tap : tap + 1, :] = jnp.sum(acc[b], axis=0, keepdims=True)

    for c in range(CHUNKS):
        units = slice(SMALL + c * SMALL_TALL, SMALL + (c + 1) * SMALL_TALL)
        total.away[units] = small[1 - core, c].reshape(SMALL_TALL, 16, 128)
        total.own[units] = small[core, c].reshape(SMALL_TALL, 16, 128)
    total.pair(2)
    total.relay(1)
    total.scatter_first(2)
    for step in (1, 2):
        for part in range(3):
            total.scatter(part, step)
        if step == 1:
            total.loss_next(2)
    for step in (2, 1):
        for part in range(3):
            total.gather(part, step)
    total.gather_last()
    loss_ref[...] = total.loss_take(3)

    @pl.loop(0, CHUNKS - 1)
    def _(c):
        for copy in halo(c):
            copy.wait_send()

    for c in list(thin) + sent + back + total.open:
        c.wait_send()


def gradients(state, conv_kernel, gain, up, down_t, head_t, target, field_weight):
    f32, bf16 = jnp.float32, jnp.bfloat16
    vmem = pl.BlockSpec(memory_space=pltpu.VMEM)
    anywhere = pl.BlockSpec(memory_space=pl.ANY)
    V = pltpu.VMEM
    dma = pltpu.SemaphoreType.DMA
    work = dict(
        win=V((CHUNKS, 6, 176, 128), f32),
        ck=V((CHUNKS, 25, 128), f32),
        gn=V((CHUNKS, 1, 128), f32),
        su=V((CHUNKS, CELLS, 128), f32),
        nr=V((CHUNKS, CELLS, 128), f32),
        inv=V((CELLS, 1), f32),
        sc=V((CELLS, 768), bf16),
        rd=V((CELLS, 768), bf16),
        pre=V((CELLS, HID), f32),
        slope=V((CELLS, HID), f32),
        hid=V((CELLS, HID), bf16),
        hp=V((FIELDS, 768), bf16),
        fcs=V((CELLS, FIELDS), f32),
        fs=V((MEMBERS, BLOCK, FIELDS), f32),
        fr=V((MEMBERS, BLOCK, FIELDS), f32),
        truth=V((MEMBERS, BLOCK, FIELDS), f32),
        co_s=V((MEMBERS, BLOCK, FIELDS), bf16),
        co_r=V((MEMBERS, BLOCK, FIELDS), bf16),
        co=V((CELLS, FIELDS), bf16),
        dp=V((CELLS, HID), bf16),
        dsum=V((CHUNKS, CELLS, 128), f32),
        dsc=V((CHUNKS, CELLS, 128), f32),
        small=V((2, CHUNKS, 64, 128), f32),
        thin_s=V((8, LON), f32),
        thin_r=V((2, 8, LON), f32),
        up=V((C, HID), bf16),
        down_t=V((C, HID), bf16),
        drr=V((CELLS, 768), bf16),
        halo_s=dma((2, CHUNKS)),
        halo_r=dma((2, CHUNKS)),
        fc_s=dma((MEMBERS - 1,)),
        fc_r=dma((MEMBERS - 1,)),
        ct_s=dma((MEMBERS - 1,)),
        ct_r=dma((MEMBERS - 1,)),
        wt=dma((2,)),
    )
    refs, tree = jax.tree.flatten((work, total_scratch()))

    def kernel(*args):
        step_kernel(*args[:10], *jax.tree.unflatten(tree, args[10:]))

    return pl.pallas_call(
        kernel,
        out_shape=(
            jax.ShapeDtypeStruct((2, UNITS, 16, 128), bf16),
            jax.ShapeDtypeStruct((8, 128), f32),
        ),
        in_specs=[vmem, vmem, vmem, anywhere, anywhere, vmem, vmem, vmem],
        out_specs=(vmem, vmem),
        scratch_shapes=refs,
        compiler_params=pltpu.CompilerParams(
            collective_id=0, has_side_effects=True, vmem_limit_bytes=58 * 1024 * 1024
        ),
    )(state, conv_kernel, gain, up, down_t, head_t, target, field_weight)


def unpack_kernel(g_ref, loss, up_ref, down_ref, head_ref, kern_ref, gain_ref, loss_ref, small):
    for m, out in enumerate((down_ref, up_ref)):
        for core in range(2):
            for j in range(WIDE):
                start = m * HALF + j * TALL
                piece = g_ref[core, start : start + TALL].astype(jnp.float32)
                lane = (core * WIDE + j) * 128
                out[0:640, lane : lane + 128] = piece.reshape(640, 128)
    for core in range(2):
        for c in range(CHUNKS):
            start = SMALL + c * SMALL_TALL
            piece = g_ref[core, start : start + SMALL_TALL].astype(jnp.float32)
            small[core, :, c * 128 : (c + 1) * 128] = piece.reshape(64, 128)
    head_ref[0:64, :] = small[0, :, 0:641]
    head_ref[64:72, :] = small[1, 0:8, 0:641]
    kern_ref[...] = small[1, 8:33, 0:641]
    gain_ref[...] = small[1, 33:34, 0:641]
    loss_ref[...] = loss[0:1, 0:1]
    for r, out in ((34, up_ref), (39, down_ref)):
        edge = small[1, 32:56, :]
        out[:, 1280:1282] = jnp.transpose(edge)[0:641, r - 32 : r - 30]
        out[640:641, 0:640] = small[1, r + 2 : r + 3, 0:640]
        out[640:641, 640:1280] = small[1, r + 3 : r + 4, 0:640]


def unpacked(g, loss):
    vmem = pl.BlockSpec(memory_space=pltpu.VMEM)
    shapes = ((C, HID), (C, HID), (FIELDS, C), (25, C), (1, C), (1, 1))
    return pl.pallas_call(
        unpack_kernel,
        out_shape=tuple(jax.ShapeDtypeStruct(s, jnp.float32) for s in shapes),
        in_specs=[vmem, vmem],
        out_specs=(vmem,) * 6,
        scratch_shapes=[pltpu.VMEM((2, 64, 768), jnp.float32)],
        compiler_params=pltpu.CompilerParams(vmem_limit_bytes=48 * 1024 * 1024),
    )(g, loss)


def local(
    state, conv_kernel, norm_gain, up_weight, down_weight, field_head_weight, target, field_weight
):
    total, loss = gradients(
        jnp.transpose(state[0], (1, 2, 0)),
        conv_kernel,
        norm_gain,
        up_weight,
        down_weight.T,
        field_head_weight.T,
        target,
        field_weight[None],
    )
    up, down_t, head_t, kern, gain_row, loss = unpacked(total, loss)
    return (loss.reshape(()), kern, gain_row.reshape(C), up, down_t.T, head_t.T)


def solution(mesh):
    finer = Mesh(mesh.devices.reshape(4, 2, 2, 2, 8), AXES)
    mem, lat = AXES[:3], AXES[3:]
    in_specs = (P(mem, None, lat, None), P(), P(), P(), P(), P(), P(None, lat, None), P())
    out_specs = (P(), P(), P(), P(), P(), P())
    return jax.shard_map(local, mesh=finer, in_specs=in_specs, out_specs=out_specs, check_vma=False)
```

time: 124 us -> 109 us (0.88)
  Pallas kernels: 119 us -> 105 us
    pallas_call x3 -> x2, Pallas kernels: 119 us -> 105 us  [the longest x1 102 us: gradients(): pl.pallas_call(kernel, out_shape=(jax.ShapeDtypeStruct((2, UNITS, 16, 128...]
    unnamed x2 -> x4, local copies, waits for them, and re-layouts: 0.68 us -> 2.66 us
    another operation x1 -> x0, local copies, waits for them, and re-layouts: 1.33 us -> none
    broadcast_in_dim x1 -> x0, local copies, waits for them, and re-layouts: 1.27 us -> none  [local(): norm_gain[None]]
where the time goes in v3:
time: 109 us
  Pallas kernels  105 us (96%)
  local copies, waits for them, and re-layouts  2.66 us (2%)
    pallas_call x1, Pallas kernels, gradients(): pl.pallas_call(kernel, out_shape=(jax.ShapeDtypeStruct((2, UNITS, 16, 128...  102 us
    pallas_call x1, Pallas kernels, unpacked(): pl.pallas_call(unpack_kernel, out_shape=tuple((jax.ShapeDtypeStruct(s, jn...  3.56 us
    unnamed x4, local copies, waits for them, and re-layouts  2.66 us

profile of v3, /device:TPU:1, one launch (start us, length us, event | category | flops | bytes accessed | tf_op | source)
XLA Modules:
  0.0 109.1 jit_solution(3154298976156649639)
XLA Ops:
  0.6 101.6 %shard_map.127 = (bf16[2,424,16,128]{3,2,1,0:T(8,128)(2,1)}, f32[8,128]{1,0:T(8,128)}) custom-call(f32[2,160,641]{2,1,0:T(8,128)} %bitcast.10, f32[25,641]{1,0:T(8,128)} %args_1_.4, f32[641]{0:T(1024)} %args_2_.4, bf16[641,1282]{1,0:T(8,128)(2,1)} %args_3_.4, bf16[641,1282]{1,0:T(8,128)(2,1)} %bitcast.9, bf16[72,641]{1,0:T(8,128)(2,1)} %bitcast.11, ...), custom_call_target="tpu_custom_call" | custom-call | tf_op jit(solution)/shard_map/pallas_call | solution.py:716
  102.3 0.0 copy-start
  102.3 2.0 %copy-done = bf16[2,424,16,128]{3,2,1,0:T(8,128)(2,1)S(1)} copy-done((bf16[2,424,16,128]{3,2,1,0:T(8,128)(2,1)S(1)}, bf16[2,424,16,128]{3,2,1,0:T(8,128)(2,1)}, u32[]{:S(2)}) %copy-start) | copy-done | bytes 3473432
  104.3 0.0 copy-start.1
  104.3 0.7 copy-done.1
  104.9 3.6 %shard_map.128 = (f32[641,1282]{1,0:T(8,128)}, f32[641,1282]{1,0:T(8,128)}, f32[72,641]{1,0:T(8,128)}, f32[25,641]{1,0:T(8,128)}, f32[1,641]{1,0:T(1,128)S(1)}, /*index=5*/f32[1,1]{1,0:T(1,128)}) custom-call(bf16[2,424,16,128]{3,2,1,0:T(8,128)(2,1)S(1)} %copy-done, f32[8,128]{1,0:T(8,128)S(1)} %copy-done.1), custom_call_target="tpu_custom_call" | custom-call | tf_op jit(solution)/shard_map/pallas_call | solution.py:759
  108.5 0.6 reduce
Async XLA Ops:
  102.3 2.0 %copy-start = (bf16[2,424,16,128]{3,2,1,0:T(8,128)(2,1)S(1)}, bf16[2,424,16,128]{3,2,1,0:T(8,128)(2,1)}, u32[]{:S(2)}) copy-start(bf16[2,424,16,128]{3,2,1,0:T(8,128)(2,1)} %get-tuple-element.14.g_ref) | copy-start | bytes 10420228
  104.3 0.7 copy-start.1

commit v4 on v3

--- a/solution.py
+++ b/solution.py
@@ -34,10 +34,11 @@
 SMALL_TALL = 4
 UNITS = SMALL + SMALL_TALL * CHUNKS
 SIZE = {"x": 4, "y": 4, "z": 8}
-PARTS = ((0, 192, "xyz", True), (192, 192, "yxz", True), (384, 40, "xyz", False))
-
-
-def steps_of(size, order):
+PARTS = ((0, 100, "xy"), (100, 100, "yx"), (200, 100, "xy"), (300, 100, "yx"), (400, 24, "xy"))
+GROUPS = ((0, 1), (2, 3, 4))
+
+
+def levels_of(size, order):
     levels = []
     for a in order:
         size = -(-size // SIZE[a])
@@ -45,7 +46,15 @@
     return levels
 
 
-PLANS = tuple((off, size, steps_of(size, order), relay) for off, size, order, relay in PARTS)
+PLANS = tuple((off, size, levels_of(size, order)) for off, size, order in PARTS)
+
+
+def group_of(group):
+    starts, at = {}, 0
+    for k in GROUPS[group]:
+        starts[k] = at
+        at += PLANS[k][2][1][2]
+    return starts, at, -(-at // SIZE["z"])
 
 
 def contract(left, right, dims):
@@ -77,9 +86,9 @@
 
 
 class Total:
-    def __init__(self, g_ref, own, away, core_in, parts, loss_in, sems):
+    def __init__(self, g_ref, own, away, core_in, parts, groups, loss_in, sems):
         self.g, self.own, self.away, self.core_in, self.parts, self.loss_in = g_ref, own, away, core_in, parts, loss_in
-        self.sems = sems
+        self.sems, self.groups, self.last = sems, groups, []
         self.core = lax.axis_index("mem_2")
         self.sibling = {"mem_2": 1 - self.core}
         self.at = {
@@ -138,175 +147,114 @@
     def held(self, start, count):
         return self.own[pl.ds(start, count)] + self.core_in[pl.ds(start, count)]
 
-    def scatter_first(self, k):
-        off, size, levels, relay = PLANS[k]
-        a, n, u = levels[0]
-        send, recv = self.parts[k][0][:2]
-        self.first[k].wait_recv()
-        send[...] = self.held(off, size).astype(jnp.bfloat16)
-        if not relay:
-            self.scatter_sends(k, 0)
-            return
-        s, r = self.sems["relay"]
-        h = u // 2
-        me = self.at[a]
-        up, down, far = (me + 1) % n, (me + n - 1) % n, (me + 2) % n
-        into = self.parts[k][0][4]
-        dev_up, dev_down = device_at(a, up), device_at(a, down)
-        b = lambda i, src, dst, dev: self.begin(src, dst, s.at[k, i], r.at[k, i], dev)
-        self.running[k] = [
-            b(0, send.at[pl.ds(far * u, h)], into.at[0], dev_up),
-            b(1, send.at[pl.ds(far * u + h, h)], into.at[1], dev_down),
-            b(2, send.at[pl.ds(up * u + h, h)], recv.at[0, pl.ds(h, h)], dev_up),
-            b(3, send.at[pl.ds(down * u, h)], recv.at[1, pl.ds(0, h)], dev_down),
-        ]
-
-    def relay(self, k):
-        off, size, levels, _ = PLANS[k]
-        a, n, u = levels[0]
-        recv, into, outof = self.parts[k][0][1], self.parts[k][0][4], self.parts[k][0][5]
-        s, r = self.sems["relay"]
-        h = u // 2
-        me = self.at[a]
-        up, down = (me + 1) % n, (me + n - 1) % n
-        for i, (dev, start, half) in enumerate(((up, off + up * u, 0), (down, off + down * u + h, h))):
-            self.running[k][i].wait_recv()
-            outof[i] = (self.held(start, h) + into[i].astype(jnp.float32)).astype(jnp.bfloat16)
-            self.running[k].append(
-                self.begin(outof.at[i], recv.at[i, pl.ds(half, h)], s.at[k, 4 + i], r.at[k, 4 + i], device_at(a, dev))
+    def arrive(self, key):
+        for c in self.running[key]:
+            c.wait_recv()
+        self.running[key] = []
+
+    def spread(self, key, send, recv, sems, row, axis, u):
+        s, r = self.sems[sems]
+        n = SIZE[axis]
+        self.running[key] = []
+        for d in range(1, n):
+            p = (self.at[axis] + d) % n
+            self.running[key].append(
+                self.begin(send.at[pl.ds(p * u, u)], recv.at[d - 1], s.at[row, d - 1], r.at[row, d - 1], device_at(axis, p))
             )
-        self.running[k] = self.running[k][2:]
-
-    def scatter_sends(self, k, level):
-        a, n, u = PLANS[k][2][level]
-        send, recv = self.parts[k][level][:2]
-        s, r = self.sems["scatter"]
-        self.running[k] = []
-        for d in range(1, n):
-            p = (self.at[a] + d) % n
-            self.running[k].append(
-                self.begin(
-                    send.at[pl.ds(p * u, u)], recv.at[d - 1], s.at[k, level, d - 1], r.at[k, level, d - 1], device_at(a, p)
-                )
-            )
-
-    def gathered_sum(self, k, level):
-        off, size, levels, relay = PLANS[k]
-        a, n, u = levels[level]
-        recv, total = self.parts[k][level][1:3]
-        for c in self.running[k]:
-            c.wait_recv()
-        me = self.at[a]
-        value = self.held(off + me * u, u) if level == 0 else total[pl.ds(me * u, u)]
-        for d in range(2 if relay and level == 0 else n - 1):
-            value = value + recv[d].astype(jnp.float32)
-        return value
-
-    def scatter(self, k, level):
-        a, n, u = PLANS[k][2][level]
-        below = PLANS[k][2][level - 1][2]
-        send, recv, total = self.parts[k][level][:3]
-        total[0:below] = self.gathered_sum(k, level - 1)
-        if n * u > below:
-            total[below:] = jnp.zeros((n * u - below, 16, 128), jnp.float32)
-        send[...] = total[...].astype(jnp.bfloat16)
-        self.scatter_sends(k, level)
-
-    def gather(self, k, level):
-        a, n, u = PLANS[k][2][level]
-        into = self.parts[k][level][3]
-        me = self.at[a]
-        mine = pl.ds(me * u, u)
-        s, r = self.sems["gather"]
-        if level == 2:
-            into[mine] = self.gathered_sum(k, 2).astype(jnp.bfloat16)
-            source = into.at[mine]
-        else:
-            below = self.parts[k][level + 1][3]
-            for c in self.running[k]:
-                c.wait_recv()
-            into[mine] = below[0:u]
-            source = below.at[pl.ds(0, u)]
-        self.running[k] = [
+
+    def share(self, key, source, into, sems, row, axis, start):
+        s, r = self.sems[sems]
+        n = SIZE[axis]
+        self.running[key] = [
             self.begin(
-                source, into.at[mine], s.at[k, level, d - 1], r.at[k, level, d - 1], device_at(a, (me + d) % n)
+                source, into.at[start], s.at[row, d - 1], r.at[row, d - 1], device_at(axis, (self.at[axis] + d) % n)
             )
             for d in range(1, n)
         ]
+
+    def scatter_0(self, k):
+        off, size, levels = PLANS[k]
+        a, n, u = levels[0]
+        send, recv = self.parts[k][:2]
+        self.first[k].wait_recv()
+        send[...] = self.held(off, size).astype(jnp.bfloat16)
+        self.spread(k, send, recv, "scatter_0", k, a, u)
+
+    def scatter_1(self, k):
+        off, size, levels = PLANS[k]
+        a, n, below = levels[0]
+        b, m, u = levels[1]
+        came, total, send, recv = self.parts[k][1:5]
+        self.arrive(k)
+        value = self.held(off + self.at[a] * below, below)
+        for d in range(n - 1):
+            value = value + came[d].astype(jnp.float32)
+        total[0:below] = value
+        if m * u > below:
+            total[below:] = jnp.zeros((m * u - below, 16, 128), jnp.float32)
+        send[...] = total[...].astype(jnp.bfloat16)
+        self.spread(k, send, recv, "scatter_1", k, b, u)
+
+    def scatter_2(self, group):
+        starts, used, u = group_of(group)
+        total, send, recv = self.groups[group][:3]
+        if 8 * u > used:
+            total[used:] = jnp.zeros((8 * u - used, 16, 128), jnp.float32)
+        for k in GROUPS[group]:
+            b, m, below = PLANS[k][2][1]
+            held, came = self.parts[k][2], self.parts[k][4]
+            self.arrive(k)
+            value = held[pl.ds(self.at[b] * below, below)]
+            for d in range(m - 1):
+                value = value + came[d].astype(jnp.float32)
+            total[starts[k] : starts[k] + below] = value
+        send[...] = total[...].astype(jnp.bfloat16)
+        self.spread(("z", group), send, recv, "scatter_2", group, "z", u)
+
+    def gather_2(self, group):
+        starts, used, u = group_of(group)
+        total, send, recv, into = self.groups[group]
+        self.arrive(("z", group))
+        mine = pl.ds(self.at["z"] * u, u)
+        value = total[mine]
+        for d in range(7):
+            value = value + recv[d].astype(jnp.float32)
+        into[mine] = value.astype(jnp.bfloat16)
+        self.share(("z", group), into.at[mine], into, "gather_2", group, "z", mine)
+
+    def gather_1(self, k):
+        group = 0 if k in GROUPS[0] else 1
+        b, m, u = PLANS[k][2][1]
+        start = group_of(group)[0][k]
+        source, into = self.groups[group][3], self.parts[k][5]
+        self.arrive(("z", group))
+        mine = pl.ds(self.at[b] * u, u)
+        into[mine] = source[start : start + u]
+        self.share(k, source.at[pl.ds(start, u)], into, "gather_1", k, b, mine)
 
     def to_sibling(self, k, i, start, count):
         s, r = self.sems["back"]
         piece = self.g.at[self.core, pl.ds(start, count)]
         self.last.append(self.begin(piece, piece, s.at[k, i], r.at[k, i], self.sibling))
 
-    last = None
-
-    def gather_last(self):
-        self.last = []
-        s, r = self.sems["gather"]
-        s2, r2 = self.sems["relay_back"]
-        flights = {}
-        for k, (off, size, levels, relay) in enumerate(PLANS):
-            a, n, u = levels[0]
-            me = self.at[a]
-            below = self.parts[k][1][3]
-            for c in self.running[k]:
-                c.wait_recv()
-            mine = pl.ds(off + me * u, u)
-            self.g[self.core, mine] = below[0:u]
-            if relay:
-                h = u // 2
-                up, down = device_at(a, (me + 1) % n), device_at(a, (me + n - 1) % n)
-                lo, hi = pl.ds(off + me * u, h), pl.ds(off + me * u + h, h)
-                b = lambda i, part, src, dev: self.begin(
-                    src, self.g.at[self.core, part], s2.at[k, i], r2.at[k, i], dev
-                )
-                flights[k] = [
-                    b(0, lo, below.at[pl.ds(0, h)], up),
-                    b(1, hi, below.at[pl.ds(h, h)], down),
-                    b(2, hi, below.at[pl.ds(h, h)], up),
-                    b(3, lo, below.at[pl.ds(0, h)], down),
-                ]
-            else:
-                flights[k] = [
-                    self.begin(
-                        below.at[pl.ds(0, u)],
-                        self.g.at[self.core, mine],
-                        s.at[k, 0, d - 1],
-                        r.at[k, 0, d - 1],
-                        device_at(a, (me + d) % n),
-                    )
-                    for d in range(1, n)
-                ]
-            self.to_sibling(k, 0, off + me * u, u)
-        for k, (off, size, levels, relay) in enumerate(PLANS):
-            a, n, u = levels[0]
-            me = self.at[a]
-            if not relay:
-                continue
-            h = u // 2
-            up, down = (me + 1) % n, (me + n - 1) % n
-            for i, (start, dev) in enumerate(((off + down * u, up), (off + up * u + h, down))):
-                flights[k][i].wait_recv()
-                piece = self.g.at[self.core, pl.ds(start, h)]
-                flights[k].append(
-                    self.begin(piece, piece, s2.at[k, 4 + i], r2.at[k, 4 + i], device_at(a, dev))
-                )
-                self.to_sibling(k, 1 + i, start, h)
-        for k, (off, size, levels, relay) in enumerate(PLANS):
-            a, n, u = levels[0]
-            me = self.at[a]
-            h = u // 2
-            up, down, far = (me + 1) % n, (me + n - 1) % n, (me + 2) % n
-            if relay:
-                starts = (off + down * u + h, off + up * u, off + far * u, off + far * u + h)
-                for i, start in enumerate(starts):
-                    flights[k][2 + i].wait_recv()
-                    self.to_sibling(k, 3 + i, start, h)
-            else:
-                for d in range(1, n):
-                    flights[k][d - 1].wait_recv()
-                    self.to_sibling(k, d, off + ((me + n - d) % n) * u, u)
+    def gather_0(self, k):
+        off, size, levels = PLANS[k]
+        a, n, u = levels[0]
+        source = self.parts[k][5]
+        self.arrive(k)
+        mine = pl.ds(off + self.at[a] * u, u)
+        self.g[self.core, mine] = source[0:u]
+        self.share(k, source.at[pl.ds(0, u)], self.g.at[self.core], "gather_0", k, a, mine)
+        self.to_sibling(k, 0, off + self.at[a] * u, u)
+
+    def hand_over(self, k):
+        off, size, levels = PLANS[k]
+        a, n, u = levels[0]
+        for d in range(1, n):
+            self.running[k][d - 1].wait_recv()
+            self.to_sibling(k, d, off + ((self.at[a] + n - d) % n) * u, u)
+
+    def finish(self):
         for c in self.last:
             c.wait_recv()
 
@@ -314,38 +262,45 @@
 def total_scratch():
     bf16, f32 = jnp.bfloat16, jnp.float32
     V = pltpu.VMEM
-    parts = []
-    for off, size, levels, relay in PLANS:
-        part = []
-        for level, (a, n, u) in enumerate(levels):
-            relays = relay and level == 0
-            one = [
-                V((n * u, 16, 128), bf16),
-                V((2 if relays else n - 1, u, 16, 128), bf16),
-                V((n * u if level else 1, 16, 128), f32),
-                V((n * u if level else 1, 16, 128), bf16),
+    parts, groups = [], []
+    for off, size, levels in PLANS:
+        (a, n, u), (b, m, v) = levels
+        parts.append(
+            [
+                V((size, 16, 128), bf16),
+                V((n - 1, u, 16, 128), bf16),
+                V((m * v, 16, 128), f32),
+                V((m * v, 16, 128), bf16),
+                V((m - 1, v, 16, 128), bf16),
+                V((m * v, 16, 128), bf16),
             ]
-            if relays:
-                one += [V((2, u // 2, 16, 128), bf16), V((2, u // 2, 16, 128), bf16)]
-            part.append(one)
-        parts.append(part)
+        )
+    for group in range(len(GROUPS)):
+        u = group_of(group)[2]
+        groups.append(
+            [V((8 * u, 16, 128), f32), V((8 * u, 16, 128), bf16), V((7, u, 16, 128), bf16), V((8 * u, 16, 128), bf16)]
+        )
     dma = pltpu.SemaphoreType.DMA
-    sems = {
-        "pair": (dma((3,)), dma((3,))),
-        "relay": (dma((3, 6)), dma((3, 6))),
-        "relay_back": (dma((3, 6)), dma((3, 6))),
-        "scatter": (dma((3, 3, 7)), dma((3, 3, 7))),
-        "gather": (dma((3, 3, 7)), dma((3, 3, 7))),
-        "back": (dma((3, 7)), dma((3, 7))),
-        "loss": (dma((14,)), dma((14,))),
-    }
+    count = len(PLANS)
+    pairs = dict(
+        pair=(count,),
+        scatter_0=(count, 3),
+        scatter_1=(count, 3),
+        scatter_2=(2, 7),
+        gather_2=(2, 7),
+        gather_1=(count, 3),
+        gather_0=(count, 3),
+        back=(count, 4),
+        loss=(14,),
+    )
     return dict(
         own=V((UNITS, 16, 128), f32),
         away=V((UNITS, 16, 128), f32),
         core_in=V((UNITS, 16, 128), f32),
         parts=parts,
+        groups=groups,
         loss_in=V((18, 8, 128), f32),
-        sems=sems,
+        sems={name: (dma(shape), dma(shape)) for name, shape in pairs.items()},
     )
 
 
@@ -570,13 +525,15 @@
         dsum[c] = d_output[:, c * 128 : (c + 1) * 128]
     drr[...] = d_output.astype(bf16)
 
-    def half_grad(base, left, right, which, out):
-        for s, wide in ((0, 256), (256, 256), (512, 128)):
+    def half_grad(base, left, right, which, out, then=()):
+        for i, (s, wide) in enumerate(((0, 256), (256, 256), (512, 128))):
             columns = pl.ds(pl.multiple_of(which * 640 + s, 128), wide)
             part = contract(left[:, 0:640], right[:, columns], (0, 0))
             for h in range(wide // 128):
                 j = base + (s // 128 + h) * TALL
                 out[j : j + TALL] = part[:, h * 128 : (h + 1) * 128].reshape(TALL, 16, 128)
+            if i in then:
+                total.pair(then[i])
 
     def edge_grad(left, right, r):
         line = contract(left[:, 640:641], right[...], (0, 0))
@@ -587,8 +544,7 @@
             small[1, c, r : r + 2, :] = edge[:, c * 128 : (c + 1) * 128]
 
     core = total.core
-    half_grad(0, drr, hid, 1 - core, total.away)
-    total.pair(0)
+    half_grad(0, drr, hid, 1 - core, total.away, {1: 0, 2: 1})
     half_grad(0, drr, hid, core, total.own)
     pre[...] = jnp.dot(drr[:, 0:C], down_t[...], preferred_element_type=f32)
 
@@ -597,18 +553,19 @@
         rows = pl.ds(pl.multiple_of(r * 16, 16), 16)
         dp[rows, :] = (pre[rows, :] * slope[rows, :]).astype(bf16)
 
-    half_grad(HALF, sc, dp, 1 - core, total.away)
-    total.pair(1)
-    total.scatter_first(0)
+    total.scatter_0(0)
+    total.scatter_0(1)
+    half_grad(HALF, sc, dp, 1 - core, total.away, {1: 2, 2: 3})
     half_grad(HALF, sc, dp, core, total.own)
     total.loss_next(0)
-    edge_grad(drr, hid, 39)
-    edge_grad(sc, dp, 34)
     head_grad = contract(co[...], rd[...], (0, 0))
     for c in range(CHUNKS):
         small[0, c, 0:64, :] = head_grad[0:64, c * 128 : (c + 1) * 128]
         small[1, c, 0:8, :] = head_grad[64:72, c * 128 : (c + 1) * 128]
-    total.scatter_first(1)
+    total.scatter_0(2)
+    total.scatter_0(3)
+    edge_grad(drr, hid, 39)
+    edge_grad(sc, dp, 34)
     put(dsc, contract(dp[...], up[...], (1, 1)))
     mean_a = jnp.zeros((CELLS, 128), f32)
     mean_b = jnp.zeros((CELLS, 128), f32)
@@ -622,7 +579,8 @@
     for c in range(CHUNKS):
         dsum[c] = dsum[c] + inv[...] * (dsc[c] * gn[c] - mean_a - nr[c] * mean_b)
 
-    total.relay(0)
+    total.scatter_1(0)
+    total.scatter_1(1)
     total.loss_next(1)
 
     @pl.loop(0, CHUNKS)
@@ -642,18 +600,28 @@
         units = slice(SMALL + c * SMALL_TALL, SMALL + (c + 1) * SMALL_TALL)
         total.away[units] = small[1 - core, c].reshape(SMALL_TALL, 16, 128)
         total.own[units] = small[core, c].reshape(SMALL_TALL, 16, 128)
-    total.pair(2)
-    total.relay(1)
-    total.scatter_first(2)
-    for step in (1, 2):
-        for part in range(3):
-            total.scatter(part, step)
-        if step == 1:
-            total.loss_next(2)
-    for step in (2, 1):
-        for part in range(3):
-            total.gather(part, step)
-    total.gather_last()
+    total.pair(4)
+    total.scatter_2(0)
+    total.scatter_0(4)
+    total.scatter_1(2)
+    total.scatter_1(3)
+    total.loss_next(2)
+    total.scatter_1(4)
+    total.gather_2(0)
+    total.scatter_2(1)
+    total.gather_1(0)
+    total.gather_1(1)
+    total.gather_2(1)
+    total.gather_0(0)
+    total.gather_0(1)
+    total.gather_1(2)
+    total.gather_1(3)
+    total.gather_1(4)
+    for part in (2, 3, 4):
+        total.gather_0(part)
+    for part in range(5):
+        total.hand_over(part)
+    total.finish()
     loss_ref[...] = total.loss_take(3)
 
     @pl.loop(0, CHUNKS - 1)
@@ -668,7 +636,7 @@
 def gradients(state, conv_kernel, gain, up, down_t, head_t, target, field_weight):
     f32, bf16 = jnp.float32, jnp.bfloat16
     vmem = pl.BlockSpec(memory_space=pltpu.VMEM)
-    anywhere = pl.BlockSpec(memory_space=pl.ANY)
+    anywhere = pl.BlockSpec(memory_space=pltpu.HBM)
     V = pltpu.VMEM
     dma = pltpu.SemaphoreType.DMA
     work = dict(
@@ -723,46 +691,58 @@
         out_specs=(vmem, vmem),
         scratch_shapes=refs,
         compiler_params=pltpu.CompilerParams(
-            collective_id=0, has_side_effects=True, vmem_limit_bytes=58 * 1024 * 1024
+            collective_id=0, has_side_effects=True, vmem_limit_bytes=42 * 1024 * 1024
         ),
     )(state, conv_kernel, gain, up, down_t, head_t, target, field_weight)
 
 
-def unpack_kernel(g_ref, loss, up_ref, down_ref, head_ref, kern_ref, gain_ref, loss_ref, small):
-    for m, out in enumerate((down_ref, up_ref)):
-        for core in range(2):
-            for j in range(WIDE):
-                start = m * HALF + j * TALL
-                piece = g_ref[core, start : start + TALL].astype(jnp.float32)
-                lane = (core * WIDE + j) * 128
-                out[0:640, lane : lane + 128] = piece.reshape(640, 128)
+def unpack_kernel(g_ref, loss, up_hbm, down_hbm, head_ref, kern_ref, gain_ref, loss_ref, up_ref, down_ref, small, sem):
     for core in range(2):
         for c in range(CHUNKS):
             start = SMALL + c * SMALL_TALL
             piece = g_ref[core, start : start + SMALL_TALL].astype(jnp.float32)
             small[core, :, c * 128 : (c + 1) * 128] = piece.reshape(64, 128)
-    head_ref[0:64, :] = small[0, :, 0:641]
-    head_ref[64:72, :] = small[1, 0:8, 0:641]
-    kern_ref[...] = small[1, 8:33, 0:641]
-    gain_ref[...] = small[1, 33:34, 0:641]
-    loss_ref[...] = loss[0:1, 0:1]
-    for r, out in ((34, up_ref), (39, down_ref)):
+    copies = []
+    for m, r, out, hbm in ((0, 39, down_ref, down_hbm), (1, 34, up_ref, up_hbm)):
         edge = small[1, 32:56, :]
-        out[:, 1280:1282] = jnp.transpose(edge)[0:641, r - 32 : r - 30]
+        out[:, 1280:1282] = jnp.transpose(edge)[0:C, r - 32 : r - 30]
         out[640:641, 0:640] = small[1, r + 2 : r + 3, 0:640]
         out[640:641, 640:1280] = small[1, r + 3 : r + 4, 0:640]
+        for b in range(5):
+            for core in range(2):
+                for j in range(WIDE):
+                    start = m * HALF + j * TALL + b * 8
+                    piece = g_ref[core, start : start + 8].astype(jnp.float32)
+                    lane = (core * WIDE + j) * 128
+                    out[b * 128 : (b + 1) * 128, lane : lane + 128] = piece.reshape(128, 128)
+            rows = pl.ds(b * 128, 128 if b < 4 else 129)
+            copies.append(pltpu.make_async_copy(out.at[rows], hbm.at[rows], sem.at[m * 5 + b]))
+            copies[-1].start()
+    head_ref[0:64, :] = small[0, :, 0:C]
+    head_ref[64:72, :] = small[1, 0:8, 0:C]
+    kern_ref[...] = small[1, 8:33, 0:C]
+    gain_ref[...] = small[1, 33:34, 0:C].reshape(C)
+    loss_ref[...] = loss[0:1, 0:1]
+    for c in copies:
+        c.wait()
 
 
 def unpacked(g, loss):
     vmem = pl.BlockSpec(memory_space=pltpu.VMEM)
-    shapes = ((C, HID), (C, HID), (FIELDS, C), (25, C), (1, C), (1, 1))
+    hbm = pl.BlockSpec(memory_space=pl.ANY)
+    shapes = ((C, HID), (C, HID), (FIELDS, C), (25, C), (C,), (1, 1))
     return pl.pallas_call(
         unpack_kernel,
         out_shape=tuple(jax.ShapeDtypeStruct(s, jnp.float32) for s in shapes),
         in_specs=[vmem, vmem],
-        out_specs=(vmem,) * 6,
-        scratch_shapes=[pltpu.VMEM((2, 64, 768), jnp.float32)],
-        compiler_params=pltpu.CompilerParams(vmem_limit_bytes=48 * 1024 * 1024),
+        out_specs=(hbm, hbm, vmem, vmem, vmem, vmem),
+        scratch_shapes=[
+            pltpu.VMEM((C, HID), jnp.float32),
+            pltpu.VMEM((C, HID), jnp.float32),
+            pltpu.VMEM((2, 64, 768), jnp.float32),
+            pltpu.SemaphoreType.DMA((10,)),
+        ],
+        compiler_params=pltpu.CompilerParams(vmem_limit_bytes=24 * 1024 * 1024),
     )(g, loss)
 
 
@@ -780,7 +760,7 @@
         field_weight[None],
     )
     up, down_t, head_t, kern, gain_row, loss = unpacked(total, loss)
-    return (loss.reshape(()), kern, gain_row.reshape(C), up, down_t.T, head_t.T)
+    return (loss.reshape(()), kern, gain_row, up, down_t.T, head_t.T)
 
 
 def solution(mesh):

time: 109 us -> 110 us (level)
  local copies, waits for them, and re-layouts: 2.66 us -> 8.22 us
  Pallas kernels: 105 us -> 101 us
    unnamed x4 -> x16, local copies, waits for them, and re-layouts: 2.66 us -> 8.22 us
    pallas_call x1, Pallas kernels: 102 us -> 96.5 us  [gradients(): pl.pallas_call(kernel, out_shape=(jax.ShapeDtypeStruct((2, UNITS, 16, 128...]
where the time goes in v4:
time: 110 us; the launch traced here: 109 us
  Pallas kernels  101 us (92%)
  local copies, waits for them, and re-layouts  8.22 us (7%)
    pallas_call x1, Pallas kernels, gradients(): pl.pallas_call(kernel, out_shape=(jax.ShapeDtypeStruct((2, UNITS, 16, 128...  96.5 us
    unnamed x16, local copies, waits for them, and re-layouts  8.22 us
    pallas_call x1, Pallas kernels, unpacked(): pl.pallas_call(unpack_kernel, out_shape=tuple((jax.ShapeDtypeStruct(s, jn...  4.03 us

profile of v4, /device:TPU:1, one launch (start us, length us, event | category | flops | bytes accessed | tf_op | source)
XLA Modules:
  0.0 109.5 jit_solution(10275048057677159439)
XLA Ops:
  0.6 0.0 copy-start
  0.6 1.5 %copy-done = bf16[641,1282]{1,0:T(8,128)(2,1)S(1)} copy-done((bf16[641,1282]{1,0:T(8,128)(2,1)S(1)}, bf16[641,1282]{1,0:T(8,128)(2,1)}, u32[]{:S(2)}) %copy-start) | copy-done | bytes 1643548
  2.1 0.0 copy-start.1
  2.1 1.5 %copy-done.1 = bf16[1282,641]{0,1:T(8,128)(2,1)S(1)} copy-done((bf16[1282,641]{0,1:T(8,128)(2,1)S(1)}, bf16[1282,641]{0,1:T(8,128)(2,1)}, u32[]{:S(2)}) %copy-start.1) | copy-done | bytes 1643548
  3.6 0.0 copy-start.2
  3.6 1.2 %copy-done.2 = f32[1,641,2,160]{1,3,2,0:T(8,128)S(1)} copy-done((f32[1,641,2,160]{1,3,2,0:T(8,128)S(1)}, f32[1,641,2,160]{1,3,2,0:T(8,128)}, u32[]{:S(2)}) %copy-start.2) | copy-done | bytes 820504
  4.8 0.0 copy-start.3
  4.8 0.9 copy-done.3
  5.7 0.0 copy-start.4
  5.7 0.9 copy-done.4
  6.6 0.0 copy-start.5
  6.6 0.9 copy-done.5
  7.5 0.0 copy-start.6
  7.5 0.7 copy-done.6
  8.2 0.0 copy-start.7
  8.2 0.7 copy-done.7
  8.9 96.5 %shard_map.127 = (bf16[2,424,16,128]{3,2,1,0:T(8,128)(2,1)S(1)}, f32[8,128]{1,0:T(8,128)S(1)}) custom-call(f32[2,160,641]{2,1,0:T(8,128)S(1)} %bitcast.10, f32[25,641]{1,0:T(8,128)S(1)} %copy-done.5, f32[641]{0:T(1024)S(1)} %copy-done.6, bf16[641,1282]{1,0:T(8,128)(2,1)S(1)} %copy-done, bf16[641,1282]{1,0:T(8,128)(2,1)S(1)} %bitcast.9, ...), custom_call_target="tpu_custom_call" | custom-call | tf_op jit(solution)/shard_map/pallas_call | solution.py:684
  105.4 4.0 %shard_map.128 = (f32[641,1282]{1,0:T(8,128)}, f32[641,1282]{1,0:T(8,128)}, f32[72,641]{1,0:T(8,128)}, f32[25,641]{1,0:T(8,128)}, f32[641]{0:T(1024)}, /*index=5*/f32[1,1]{1,0:T(1,128)}) custom-call(bf16[2,424,16,128]{3,2,1,0:T(8,128)(2,1)S(1)} %get-tuple-element.14.g_ref, f32[8,128]{1,0:T(8,128)S(1)} %get-tuple-element.15.loss), custom_call_target="tpu_custom_call" | custom-call | tf_op jit(solution)/shard_map/pallas_call | solution.py:734
Async XLA Ops:
  0.6 1.5 %copy-start = (bf16[641,1282]{1,0:T(8,128)(2,1)S(1)}, bf16[641,1282]{1,0:T(8,128)(2,1)}, u32[]{:S(2)}) copy-start(bf16[641,1282]{1,0:T(8,128)(2,1)} %args_3_.4) | copy-start | bytes 4930576
  2.1 1.5 %copy-start.1 = (bf16[1282,641]{0,1:T(8,128)(2,1)S(1)}, bf16[1282,641]{0,1:T(8,128)(2,1)}, u32[]{:S(2)}) copy-start(bf16[1282,641]{0,1:T(8,128)(2,1)} %param.12) | copy-start | bytes 4930576
  3.6 1.2 %copy-start.2 = (f32[1,641,2,160]{1,3,2,0:T(8,128)S(1)}, f32[1,641,2,160]{1,3,2,0:T(8,128)}, u32[]{:S(2)}) copy-start(f32[1,641,2,160]{1,3,2,0:T(8,128)} %param.8) | copy-start | bytes 2461444
  4.8 0.9 copy-start.3
  5.7 0.9 copy-start.4
  6.6 0.9 copy-start.5
  7.5 0.7 copy-start.6
  8.2 0.7 copy-start.7

commit v5 on v4

--- a/solution.py
+++ b/solution.py
@@ -305,14 +305,14 @@
 
 
 def step_kernel(
-    state,
-    conv_kernel,
-    gain,
+    state_hbm,
+    conv_hbm,
+    gain_hbm,
     up_hbm,
     down_hbm,
-    head_t,
-    target,
-    field_weight,
+    head_hbm,
+    target_hbm,
+    field_hbm,
     g_ref,
     loss_ref,
     w,
@@ -338,11 +338,30 @@
     greeted = [above, below] + others + total.peers()
     for dev in greeted:
         pl.semaphore_signal(barrier, inc=1, device_id=dev, device_id_type=MESH_ID)
-    weights = [pltpu.make_async_copy(up_hbm, up, wt.at[0]), pltpu.make_async_copy(down_hbm, down_t, wt.at[1])]
-    for c in weights:
+    state, conv_kernel, gain, head_t, target, field_weight = (
+        w[i] for i in ("state", "conv_kernel", "gain", "head_t", "target", "field_weight")
+    )
+    loads = [
+        pltpu.make_async_copy(src, dst, wt.at[i])
+        for i, (src, dst) in enumerate(
+            (
+                (state_hbm, state),
+                (conv_hbm, conv_kernel),
+                (gain_hbm, gain),
+                (head_hbm, head_t),
+                (target_hbm, target),
+                (field_hbm, field_weight),
+                (up_hbm, up),
+                (down_hbm, down_t),
+            )
+        )
+    ]
+    for c in loads:
         c.start()
+    weights = loads[6:]
 
     win[CHUNKS - 1] = jnp.zeros((6, 176, 128), f32)
+    loads[0].wait()
     for c in range(CHUNKS - 1):
         win[c, 2:4, 8:168, :] = state[:, :, c * 128 : (c + 1) * 128]
     win[CHUNKS - 1, 2:4, 8:168, 0:1] = state[:, :, 640:641]
@@ -370,6 +389,8 @@
         for copy in halo(c):
             copy.start()
 
+    for c in loads[1:6]:
+        c.wait()
     ck[CHUNKS - 1] = jnp.zeros((25, 128), f32)
     put(ck, conv_kernel[...])
     gn[CHUNKS - 1] = jnp.zeros((1, 128), f32)
@@ -674,7 +695,13 @@
         fc_r=dma((MEMBERS - 1,)),
         ct_s=dma((MEMBERS - 1,)),
         ct_r=dma((MEMBERS - 1,)),
-        wt=dma((2,)),
+        wt=dma((8,)),
+        state=V((ROWS, LON, C), f32),
+        conv_kernel=V((25, C), f32),
+        gain=V((C,), f32),
+        head_t=V((FIELDS, C), bf16),
+        target=V((FIELDS, ROWS, LON), f32),
+        field_weight=V((1, FIELDS), f32),
     )
     refs, tree = jax.tree.flatten((work, total_scratch()))
 
@@ -687,13 +714,18 @@
             jax.ShapeDtypeStruct((2, UNITS, 16, 128), bf16),
             jax.ShapeDtypeStruct((8, 128), f32),
         ),
-        in_specs=[vmem, vmem, vmem, anywhere, anywhere, vmem, vmem, vmem],
+        in_specs=[anywhere] * 8,
         out_specs=(vmem, vmem),
         scratch_shapes=refs,
         compiler_params=pltpu.CompilerParams(
-            collective_id=0, has_side_effects=True, vmem_limit_bytes=42 * 1024 * 1024
+            collective_id=0, has_side_effects=True, vmem_limit_bytes=48 * 1024 * 1024
         ),
-    )(state, conv_kernel, gain, up, down_t, head_t, target, field_weight)
+    )(
+        *(
+            pltpu.with_memory_space_constraint(a, pltpu.HBM)
+            for a in (state, conv_kernel, gain, up, down_t, head_t, target, field_weight)
+        )
+    )
 
 
 def unpack_kernel(g_ref, loss, up_hbm, down_hbm, head_ref, kern_ref, gain_ref, loss_ref, up_ref, down_ref, small, sem):

time: 110 us -> 102 us (0.927)
  local copies, waits for them, and re-layouts: 8.22 us -> 0 us
    unnamed x16 -> x0, local copies, waits for them, and re-layouts: 8.22 us -> none
where the time goes in v5:
time: 102 us; the launch traced here: 101 us
  Pallas kernels  101 us (99%)
    pallas_call x1, Pallas kernels, gradients(): pl.pallas_call(kernel, out_shape=(jax.ShapeDtypeStruct((2, UNITS, 16, 128...  96.8 us
    pallas_call x1, Pallas kernels, unpacked(): pl.pallas_call(unpack_kernel, out_shape=tuple((jax.ShapeDtypeStruct(s, jn...  4.03 us

profile of v5, /device:TPU:1, one launch (start us, length us, event | category | flops | bytes accessed | tf_op | source)
XLA Modules:
  0.0 101.5 jit_solution(2611823865409614827)
XLA Ops:
  0.6 96.8 %shard_map.127 = (bf16[2,424,16,128]{3,2,1,0:T(8,128)(2,1)S(1)}, f32[8,128]{1,0:T(8,128)S(1)}) custom-call(f32[2,160,641]{2,1,0:T(8,128)} %bitcast.10, f32[25,641]{1,0:T(8,128)} %args_1_.4, f32[641]{0:T(1024)} %args_2_.4, bf16[641,1282]{1,0:T(8,128)(2,1)} %args_3_.4, bf16[641,1282]{1,0:T(8,128)(2,1)} %bitcast.9, bf16[72,641]{1,0:T(8,128)(2,1)} %bitcast.11, ...), custom_call_target="tpu_custom_call" | custom-call | tf_op jit(solution)/shard_map/pallas_call | solution.py:711
  97.4 4.0 %shard_map.128 = (f32[641,1282]{1,0:T(8,128)}, f32[641,1282]{1,0:T(8,128)}, f32[72,641]{1,0:T(8,128)}, f32[25,641]{1,0:T(8,128)}, f32[641]{0:T(1024)}, /*index=5*/f32[1,1]{1,0:T(1,128)}) custom-call(bf16[2,424,16,128]{3,2,1,0:T(8,128)(2,1)S(1)} %get-tuple-element.14.g_ref, f32[8,128]{1,0:T(8,128)S(1)} %get-tuple-element.15.loss), custom_call_target="tpu_custom_call" | custom-call | tf_op jit(solution)/shard_map/pallas_call | solution.py:766

commit v6 on v5

--- a/solution.py
+++ b/solution.py
@@ -35,7 +35,7 @@
 UNITS = SMALL + SMALL_TALL * CHUNKS
 SIZE = {"x": 4, "y": 4, "z": 8}
 PARTS = ((0, 100, "xy"), (100, 100, "yx"), (200, 100, "xy"), (300, 100, "yx"), (400, 24, "xy"))
-GROUPS = ((0, 1), (2, 3, 4))
+GROUPS = ((0, 1), (2, 3), (4,))
 
 
 def levels_of(size, order):
@@ -223,7 +223,7 @@
         self.share(("z", group), into.at[mine], into, "gather_2", group, "z", mine)
 
     def gather_1(self, k):
-        group = 0 if k in GROUPS[0] else 1
+        group = [g for g, members in enumerate(GROUPS) if k in members][0]
         b, m, u = PLANS[k][2][1]
         start = group_of(group)[0][k]
         source, into = self.groups[group][3], self.parts[k][5]
@@ -286,8 +286,8 @@
         pair=(count,),
         scatter_0=(count, 3),
         scatter_1=(count, 3),
-        scatter_2=(2, 7),
-        gather_2=(2, 7),
+        scatter_2=(3, 7),
+        gather_2=(3, 7),
         gather_1=(count, 3),
         gather_0=(count, 3),
         back=(count, 4),
@@ -585,8 +585,6 @@
         small[1, c, 0:8, :] = head_grad[64:72, c * 128 : (c + 1) * 128]
     total.scatter_0(2)
     total.scatter_0(3)
-    edge_grad(drr, hid, 39)
-    edge_grad(sc, dp, 34)
     put(dsc, contract(dp[...], up[...], (1, 1)))
     mean_a = jnp.zeros((CELLS, 128), f32)
     mean_b = jnp.zeros((CELLS, 128), f32)
@@ -603,6 +601,8 @@
     total.scatter_1(0)
     total.scatter_1(1)
     total.loss_next(1)
+    edge_grad(drr, hid, 39)
+    edge_grad(sc, dp, 34)
 
     @pl.loop(0, CHUNKS)
     def _(c):
@@ -627,20 +627,25 @@
     total.scatter_1(2)
     total.scatter_1(3)
     total.loss_next(2)
-    total.scatter_1(4)
     total.gather_2(0)
     total.scatter_2(1)
+    total.scatter_1(4)
     total.gather_1(0)
     total.gather_1(1)
+    total.scatter_2(2)
     total.gather_2(1)
     total.gather_0(0)
     total.gather_0(1)
     total.gather_1(2)
     total.gather_1(3)
+    total.gather_2(2)
+    total.gather_0(2)
+    total.gather_0(3)
     total.gather_1(4)
+    total.hand_over(0)
+    total.hand_over(1)
+    total.gather_0(4)
     for part in (2, 3, 4):
-        total.gather_0(part)
-    for part in range(5):
         total.hand_over(part)
     total.finish()
     loss_ref[...] = total.loss_take(3)
@@ -728,16 +733,30 @@
     )
 
 
-def unpack_kernel(g_ref, loss, up_hbm, down_hbm, head_ref, kern_ref, gain_ref, loss_ref, up_ref, down_ref, small, sem):
+def unpack_kernel(g_ref, loss, *refs):
+    hbm, (up_ref, down_ref, head_ref, kern_ref, gain_ref, loss_ref, small, sem) = refs[:6], refs[6:]
+    copies = []
+
+    def send(src, dst):
+        copies.append(pltpu.make_async_copy(src, dst, sem.at[len(copies)]))
+        copies[-1].start()
+
+    loss_ref[...] = loss[0:1, 0:1]
+    send(loss_ref, hbm[5])
     for core in range(2):
         for c in range(CHUNKS):
             start = SMALL + c * SMALL_TALL
             piece = g_ref[core, start : start + SMALL_TALL].astype(jnp.float32)
             small[core, :, c * 128 : (c + 1) * 128] = piece.reshape(64, 128)
-    copies = []
-    for m, r, out, hbm in ((0, 39, down_ref, down_hbm), (1, 34, up_ref, up_hbm)):
-        edge = small[1, 32:56, :]
-        out[:, 1280:1282] = jnp.transpose(edge)[0:C, r - 32 : r - 30]
+    head_ref[0:64, :] = small[0, :, 0:C]
+    head_ref[64:72, :] = small[1, 0:8, 0:C]
+    send(head_ref, hbm[2])
+    kern_ref[...] = small[1, 8:33, 0:C]
+    send(kern_ref, hbm[3])
+    gain_ref[...] = small[1, 33:34, 0:C].reshape(C)
+    send(gain_ref, hbm[4])
+    edge = jnp.transpose(small[1, 32:56, :])
+    for m, r, out, target in ((0, 39, down_ref, hbm[1]), (1, 34, up_ref, hbm[0])):
         out[640:641, 0:640] = small[1, r + 2 : r + 3, 0:640]
         out[640:641, 640:1280] = small[1, r + 3 : r + 4, 0:640]
         for b in range(5):
@@ -747,33 +766,25 @@
                     piece = g_ref[core, start : start + 8].astype(jnp.float32)
                     lane = (core * WIDE + j) * 128
                     out[b * 128 : (b + 1) * 128, lane : lane + 128] = piece.reshape(128, 128)
-            rows = pl.ds(b * 128, 128 if b < 4 else 129)
-            copies.append(pltpu.make_async_copy(out.at[rows], hbm.at[rows], sem.at[m * 5 + b]))
-            copies[-1].start()
-    head_ref[0:64, :] = small[0, :, 0:C]
-    head_ref[64:72, :] = small[1, 0:8, 0:C]
-    kern_ref[...] = small[1, 8:33, 0:C]
-    gain_ref[...] = small[1, 33:34, 0:C].reshape(C)
-    loss_ref[...] = loss[0:1, 0:1]
+            end = (b + 1) * 128 + (b == 4)
+            out[b * 128 : end, 1280:1282] = edge[b * 128 : end, r - 32 : r - 30]
+            rows = pl.ds(b * 128, end - b * 128)
+            send(out.at[rows], target.at[rows])
     for c in copies:
         c.wait()
 
 
 def unpacked(g, loss):
     vmem = pl.BlockSpec(memory_space=pltpu.VMEM)
-    hbm = pl.BlockSpec(memory_space=pl.ANY)
+    hbm = pl.BlockSpec(memory_space=pltpu.HBM)
     shapes = ((C, HID), (C, HID), (FIELDS, C), (25, C), (C,), (1, 1))
     return pl.pallas_call(
         unpack_kernel,
         out_shape=tuple(jax.ShapeDtypeStruct(s, jnp.float32) for s in shapes),
         in_specs=[vmem, vmem],
-        out_specs=(hbm, hbm, vmem, vmem, vmem, vmem),
-        scratch_shapes=[
-            pltpu.VMEM((C, HID), jnp.float32),
-            pltpu.VMEM((C, HID), jnp.float32),
-            pltpu.VMEM((2, 64, 768), jnp.float32),
-            pltpu.SemaphoreType.DMA((10,)),
-        ],
+        out_specs=(hbm,) * 6,
+        scratch_shapes=[pltpu.VMEM(s, jnp.float32) for s in shapes]
+        + [pltpu.VMEM((2, 64, 768), jnp.float32), pltpu.SemaphoreType.DMA((14,))],
         compiler_params=pltpu.CompilerParams(vmem_limit_bytes=24 * 1024 * 1024),
     )(g, loss)
 

time: 102 us -> 104 us (1.020)
  Pallas kernels: 101 us -> 104 us
    pallas_call x1, Pallas kernels: 96.8 us -> 100 us  [gradients(): pl.pallas_call(kernel, out_shape=(jax.ShapeDtypeStruct((2, UNITS, 16, 128...]
where the time goes in v6:
time: 104 us
  Pallas kernels  104 us (100%)
    pallas_call x1, Pallas kernels, gradients(): pl.pallas_call(kernel, out_shape=(jax.ShapeDtypeStruct((2, UNITS, 16, 128...  100 us
    pallas_call x1, Pallas kernels, unpacked(): pl.pallas_call(unpack_kernel, out_shape=tuple((jax.ShapeDtypeStruct(s, jn...  3.31 us

profile of v6, /device:TPU:1, one launch (start us, length us, event | category | flops | bytes accessed | tf_op | source)
XLA Modules:
  0.0 104.3 jit_solution(14618285536325126381)
XLA Ops:
  0.6 100.3 %shard_map.127 = (bf16[2,424,16,128]{3,2,1,0:T(8,128)(2,1)S(1)}, f32[8,128]{1,0:T(8,128)S(1)}) custom-call(f32[2,160,641]{2,1,0:T(8,128)} %bitcast.10, f32[25,641]{1,0:T(8,128)} %args_1_.4, f32[641]{0:T(1024)} %args_2_.4, bf16[641,1282]{1,0:T(8,128)(2,1)} %args_3_.4, bf16[641,1282]{1,0:T(8,128)(2,1)} %bitcast.9, bf16[72,641]{1,0:T(8,128)(2,1)} %bitcast.11, ...), custom_call_target="tpu_custom_call" | custom-call | tf_op jit(solution)/shard_map/pallas_call | solution.py:716
  101.0 3.3 %shard_map.128 = (f32[641,1282]{1,0:T(8,128)}, f32[641,1282]{1,0:T(8,128)}, f32[72,641]{1,0:T(8,128)}, f32[25,641]{1,0:T(8,128)}, f32[641]{0:T(1024)}, /*index=5*/f32[1,1]{1,0:T(1,128)}) custom-call(bf16[2,424,16,128]{3,2,1,0:T(8,128)(2,1)S(1)} %get-tuple-element.14.g_ref, f32[8,128]{1,0:T(8,128)S(1)} %get-tuple-element.15.loss), custom_call_target="tpu_custom_call" | custom-call | tf_op jit(solution)/shard_map/pallas_call | solution.py:781

commit v7 on v5

--- a/solution.py
+++ b/solution.py
@@ -97,6 +97,7 @@
             "z": lax.axis_index("lat_1"),
         }
         self.open = []
+        self.leaving = [[], [], [], []]
         self.first = {}
         self.running = {}
 
@@ -148,6 +149,10 @@
         return self.own[pl.ds(start, count)] + self.core_in[pl.ds(start, count)]
 
     def arrive(self, key):
+        for c in self.leaving.pop(0):
+            c.wait_send()
+        self.leaving.append(self.open)
+        self.open = []
         for c in self.running[key]:
             c.wait_recv()
         self.running[key] = []
@@ -622,6 +627,14 @@
         total.away[units] = small[1 - core, c].reshape(SMALL_TALL, 16, 128)
         total.own[units] = small[core, c].reshape(SMALL_TALL, 16, 128)
     total.pair(4)
+
+    @pl.loop(0, CHUNKS - 1)
+    def _(c):
+        for copy in halo(c):
+            copy.wait_send()
+
+    for c in list(thin) + sent + back:
+        c.wait_send()
     total.scatter_2(0)
     total.scatter_0(4)
     total.scatter_1(2)
@@ -645,12 +658,7 @@
     total.finish()
     loss_ref[...] = total.loss_take(3)
 
-    @pl.loop(0, CHUNKS - 1)
-    def _(c):
-        for copy in halo(c):
-            copy.wait_send()
-
-    for c in list(thin) + sent + back + total.open:
+    for c in sum(total.leaving, []) + total.open:
         c.wait_send()
 
 
@@ -728,16 +736,30 @@
     )
 
 
-def unpack_kernel(g_ref, loss, up_hbm, down_hbm, head_ref, kern_ref, gain_ref, loss_ref, up_ref, down_ref, small, sem):
+def unpack_kernel(g_ref, loss, *refs):
+    hbm, (up_ref, down_ref, head_ref, kern_ref, gain_ref, loss_ref, small, sem) = refs[:6], refs[6:]
+    copies = []
+
+    def send(src, dst):
+        copies.append(pltpu.make_async_copy(src, dst, sem.at[len(copies)]))
+        copies[-1].start()
+
+    loss_ref[...] = loss[0:1, 0:1]
+    send(loss_ref, hbm[5])
     for core in range(2):
         for c in range(CHUNKS):
             start = SMALL + c * SMALL_TALL
             piece = g_ref[core, start : start + SMALL_TALL].astype(jnp.float32)
             small[core, :, c * 128 : (c + 1) * 128] = piece.reshape(64, 128)
-    copies = []
-    for m, r, out, hbm in ((0, 39, down_ref, down_hbm), (1, 34, up_ref, up_hbm)):
-        edge = small[1, 32:56, :]
-        out[:, 1280:1282] = jnp.transpose(edge)[0:C, r - 32 : r - 30]
+    head_ref[0:64, :] = small[0, :, 0:C]
+    head_ref[64:72, :] = small[1, 0:8, 0:C]
+    send(head_ref, hbm[2])
+    kern_ref[...] = small[1, 8:33, 0:C]
+    send(kern_ref, hbm[3])
+    gain_ref[...] = small[1, 33:34, 0:C].reshape(C)
+    send(gain_ref, hbm[4])
+    edge = jnp.transpose(small[1, 32:56, :])
+    for m, r, out, target in ((0, 39, down_ref, hbm[1]), (1, 34, up_ref, hbm[0])):
         out[640:641, 0:640] = small[1, r + 2 : r + 3, 0:640]
         out[640:641, 640:1280] = small[1, r + 3 : r + 4, 0:640]
         for b in range(5):
@@ -747,33 +769,25 @@
                     piece = g_ref[core, start : start + 8].astype(jnp.float32)
                     lane = (core * WIDE + j) * 128
                     out[b * 128 : (b + 1) * 128, lane : lane + 128] = piece.reshape(128, 128)
-            rows = pl.ds(b * 128, 128 if b < 4 else 129)
-            copies.append(pltpu.make_async_copy(out.at[rows], hbm.at[rows], sem.at[m * 5 + b]))
-            copies[-1].start()
-    head_ref[0:64, :] = small[0, :, 0:C]
-    head_ref[64:72, :] = small[1, 0:8, 0:C]
-    kern_ref[...] = small[1, 8:33, 0:C]
-    gain_ref[...] = small[1, 33:34, 0:C].reshape(C)
-    loss_ref[...] = loss[0:1, 0:1]
+            end = (b + 1) * 128 + (b == 4)
+            out[b * 128 : end, 1280:1282] = edge[b * 128 : end, r - 32 : r - 30]
+            rows = pl.ds(b * 128, end - b * 128)
+            send(out.at[rows], target.at[rows])
     for c in copies:
         c.wait()
 
 
 def unpacked(g, loss):
     vmem = pl.BlockSpec(memory_space=pltpu.VMEM)
-    hbm = pl.BlockSpec(memory_space=pl.ANY)
+    hbm = pl.BlockSpec(memory_space=pltpu.HBM)
     shapes = ((C, HID), (C, HID), (FIELDS, C), (25, C), (C,), (1, 1))
     return pl.pallas_call(
         unpack_kernel,
         out_shape=tuple(jax.ShapeDtypeStruct(s, jnp.float32) for s in shapes),
         in_specs=[vmem, vmem],
-        out_specs=(hbm, hbm, vmem, vmem, vmem, vmem),
-        scratch_shapes=[
-            pltpu.VMEM((C, HID), jnp.float32),
-            pltpu.VMEM((C, HID), jnp.float32),
-            pltpu.VMEM((2, 64, 768), jnp.float32),
-            pltpu.SemaphoreType.DMA((10,)),
-        ],
+        out_specs=(hbm,) * 6,
+        scratch_shapes=[pltpu.VMEM(s, jnp.float32) for s in shapes]
+        + [pltpu.VMEM((2, 64, 768), jnp.float32), pltpu.SemaphoreType.DMA((14,))],
         compiler_params=pltpu.CompilerParams(vmem_limit_bytes=24 * 1024 * 1024),
     )(g, loss)
 

time: 102 us -> 101 us (level)
  no operation moved by 1% of the time
where the time goes in v7:
time: 101 us
  Pallas kernels  100 us (99%)
    pallas_call x1, Pallas kernels, gradients(): pl.pallas_call(kernel, out_shape=(jax.ShapeDtypeStruct((2, UNITS, 16, 128...  96.8 us
    pallas_call x1, Pallas kernels, unpacked(): pl.pallas_call(unpack_kernel, out_shape=tuple((jax.ShapeDtypeStruct(s, jn...  3.31 us

profile of v7, /device:TPU:1, one launch (start us, length us, event | category | flops | bytes accessed | tf_op | source)
XLA Modules:
  0.0 100.9 jit_solution(7450108071947795793)
XLA Ops:
  0.6 96.8 %shard_map.127 = (bf16[2,424,16,128]{3,2,1,0:T(8,128)(2,1)S(1)}, f32[8,128]{1,0:T(8,128)S(1)}) custom-call(f32[2,160,641]{2,1,0:T(8,128)} %bitcast.10, f32[25,641]{1,0:T(8,128)} %args_1_.4, f32[641]{0:T(1024)} %args_2_.4, bf16[641,1282]{1,0:T(8,128)(2,1)} %args_3_.4, bf16[641,1282]{1,0:T(8,128)(2,1)} %bitcast.9, bf16[72,641]{1,0:T(8,128)(2,1)} %bitcast.11, ...), custom_call_target="tpu_custom_call" | custom-call | tf_op jit(solution)/shard_map/pallas_call | solution.py:719
  97.4 3.3 %shard_map.128 = (f32[641,1282]{1,0:T(8,128)}, f32[641,1282]{1,0:T(8,128)}, f32[72,641]{1,0:T(8,128)}, f32[25,641]{1,0:T(8,128)}, f32[641]{0:T(1024)}, /*index=5*/f32[1,1]{1,0:T(1,128)}) custom-call(bf16[2,424,16,128]{3,2,1,0:T(8,128)(2,1)S(1)} %get-tuple-element.14.g_ref, f32[8,128]{1,0:T(8,128)S(1)} %get-tuple-element.15.loss), custom_call_target="tpu_custom_call" | custom-call | tf_op jit(solution)/shard_map/pallas_call | solution.py:784

commit v8 on v7

--- a/solution.py
+++ b/solution.py
@@ -636,9 +636,9 @@
     for c in list(thin) + sent + back:
         c.wait_send()
     total.scatter_2(0)
-    total.scatter_0(4)
     total.scatter_1(2)
     total.scatter_1(3)
+    total.scatter_0(4)
     total.loss_next(2)
     total.scatter_1(4)
     total.gather_2(0)

time: 101 us -> 101 us (level)
  no operation moved by 1% of the time
where the time goes in v8:
time: 101 us
  Pallas kernels  100 us (99%)
    pallas_call x1, Pallas kernels, gradients(): pl.pallas_call(kernel, out_shape=(jax.ShapeDtypeStruct((2, UNITS, 16, 128...  96.9 us
    pallas_call x1, Pallas kernels, unpacked(): pl.pallas_call(unpack_kernel, out_shape=tuple((jax.ShapeDtypeStruct(s, jn...  3.31 us

profile of v8, /device:TPU:1, one launch (start us, length us, event | category | flops | bytes accessed | tf_op | source)
XLA Modules:
  0.0 101.0 jit_solution(10119730129177531371)
XLA Ops:
  0.6 96.9 %shard_map.127 = (bf16[2,424,16,128]{3,2,1,0:T(8,128)(2,1)S(1)}, f32[8,128]{1,0:T(8,128)S(1)}) custom-call(f32[2,160,641]{2,1,0:T(8,128)} %bitcast.10, f32[25,641]{1,0:T(8,128)} %args_1_.4, f32[641]{0:T(1024)} %args_2_.4, bf16[641,1282]{1,0:T(8,128)(2,1)} %args_3_.4, bf16[641,1282]{1,0:T(8,128)(2,1)} %bitcast.9, bf16[72,641]{1,0:T(8,128)(2,1)} %bitcast.11, ...), custom_call_target="tpu_custom_call" | custom-call | tf_op jit(solution)/shard_map/pallas_call | solution.py:719
  97.6 3.3 %shard_map.128 = (f32[641,1282]{1,0:T(8,128)}, f32[641,1282]{1,0:T(8,128)}, f32[72,641]{1,0:T(8,128)}, f32[25,641]{1,0:T(8,128)}, f32[641]{0:T(1024)}, /*index=5*/f32[1,1]{1,0:T(1,128)}) custom-call(bf16[2,424,16,128]{3,2,1,0:T(8,128)(2,1)S(1)} %get-tuple-element.14.g_ref, f32[8,128]{1,0:T(8,128)S(1)} %get-tuple-element.15.loss), custom_call_target="tpu_custom_call" | custom-call | tf_op jit(solution)/shard_map/pallas_call | solution.py:784
